TPU v7x, 32 devices: a whole 2x2x4 slice. The times are simulated.
32 devices in a mesh: dp: 8 (over y, x, core), tensor: 4 (over z).
Axes of the slice: x: 2, y: 2, z: 4, core: 2. Of those that a mesh axis runs over, the one named last changes fastest.
Arguments:
- hidden_in: float32 [4096, 1024], P('dp'), may hold values from -6 to 6
- doc_ids: int32 [4096], P('dp'), may hold values from 0 to 7, never falling along the last dimension, each value on 1 to 1024 neighbouring positions
- attend_weight: bfloat16 [2, 1024, 3, 1024], P(None, 'dp', None, 'tensor'), may hold values from -0.1875 to 0.1875
- attend_bias: bfloat16 [2, 2, 1024], P(None, None, ('tensor', 'dp')), may hold values from -3 to 3
- output_weight: bfloat16 [2, 1024, 1024], P(None, ('tensor', 'dp')), may hold values from -0.75 to 0.75
- branch_bias: bfloat16 [2, 2, 1024], P(None, None, 'dp'), may hold values from -3 to 3
- expand_weight: bfloat16 [2, 1024, 4096], P(None, 'dp', 'tensor'), may hold values from -0.1875 to 0.1875
- expand_bias: bfloat16 [2, 4096], P(None, ('tensor', 'dp')), may hold values from -3 to 3
- reduce_weight: bfloat16 [2, 4096, 1024], P(None, ('tensor', 'dp')), may hold values from -0.125 to 0.125
- norm_gain: bfloat16 [2, 2, 1024], P(None, None, 'dp'), may hold values from 0.5 to 1.5
- norm_bias: bfloat16 [2, 2, 1024], P(None, None, 'dp'), may hold values from -2 to 2
- out_grad: float32 [4096, 1024], P('dp'), may hold values from -6 to 6
Outputs:
- hidden_out: float32 [4096, 1024], P('dp')
- in_grad: float32 [4096, 1024], P('dp')
- attend_wgrad: float32 [2, 1024, 3, 1024], P(None, 'dp', None, 'tensor')
- attend_bgrad: float32 [2, 2, 1024], P(None, None, ('tensor', 'dp'))
- output_wgrad: float32 [2, 1024, 1024], P(None, ('tensor', 'dp'))
- branch_bgrad: float32 [2, 2, 1024], P(None, None, 'dp')
- expand_wgrad: float32 [2, 1024, 4096], P(None, 'dp', 'tensor')
- expand_bgrad: float32 [2, 4096], P(None, ('tensor', 'dp'))
- reduce_wgrad: float32 [2, 4096, 1024], P(None, ('tensor', 'dp'))
- gain_grad: float32 [2, 2, 1024], P(None, None, 'dp')
- offset_grad: float32 [2, 2, 1024], P(None, None, 'dp')
Inputs may be any that keep to these rules, and one draw needn't show every extreme that they name: doc_ids never falls from one token to the next; each of the 8 documents holds 1 to 1024 consecutive tokens, and some document exactly 1024.
All inputs are finite; a program needn't handle non-finite values.
Results may differ from a plain program's by a relative error of at most 0.025.
Values may be sent and summed in bfloat16 or wider, within the bound.
A program may use at most 192 MiB of HBM per device.

v0:
```python
import math

import jax
import jax.numpy as jnp
from jax import lax
from jax.sharding import PartitionSpec as P

HEAD_DIM = 64
CTX = 1024


def passed_along(block, axis, distance):
    devices = range(lax.axis_size(axis))
    route = [(i - distance, i) for i in devices if i - distance in devices]
    return lax.ppermute(block, axis, route)


def contract(pattern, left_side, right_side):
    return jnp.einsum(pattern, left_side, right_side, preferred_element_type=jnp.float32)


def layer_norm(values, gain_row, offset_row):
    center = values - jnp.mean(values, axis=-1, keepdims=True)
    spread = jnp.mean(center * center, axis=-1, keepdims=True)
    return center * lax.rsqrt(spread + 1e-05) * gain_row + offset_row


def gelu_tanh(values):
    return (
        0.5
        * values
        * (1.0 + jnp.tanh(0.7978845608028654 * (values + 0.044715 * values * values * values)))
    )


def attend_forward(queries, key_block, value_block, allowed):
    factor = 1.0 / math.sqrt(queries.shape[-1])
    scores = contract("qhe,khe->hqk", queries, key_block) * factor
    unnormed = jnp.where(allowed[None], jnp.exp(scores), 0.0)
    totals = jnp.sum(unnormed, axis=-1)
    probabilities = (unnormed / totals[..., None]).astype(jnp.bfloat16)
    context = contract("hqk,khe->qhe", probabilities, value_block)
    return (context.astype(jnp.bfloat16), jnp.log(totals))


def attend_backward(queries, key_block, value_block, log_totals, out_cot, allowed):
    factor = 1.0 / math.sqrt(queries.shape[-1])
    scores = contract("qhe,khe->hqk", queries, key_block) * factor
    probabilities = jnp.where(allowed[None], jnp.exp(scores - log_totals[..., None]), 0.0)
    rounded = probabilities.astype(jnp.bfloat16)
    value_cot = contract("hqk,qhe->khe", rounded, out_cot)
    prob_cot = contract("qhe,khe->hqk", out_cot, value_block)
    row_inner = jnp.sum(probabilities * prob_cot, axis=-1, keepdims=True)
    score_cot = (probabilities * (prob_cot - row_inner) * factor).astype(jnp.bfloat16)
    query_cot = contract("hqk,khe->qhe", score_cot, key_block)
    key_cot = contract("hqk,qhe->khe", score_cot, queries)
    return (query_cot, key_cot, value_cot)


def tensor_total(partial_value):
    return lax.psum(partial_value.astype(jnp.bfloat16), "tensor").astype(jnp.float32)


def input_total(partial_value):
    return lax.psum(partial_value.astype(jnp.bfloat16), "tensor").astype(jnp.float32)


def forward_layer(hidden, params, allowed, reach_back, head_count):
    attend_w, attend_b, output_w, branch_b, expand_w, expand_b, reduce_w, gain_pair, offset_pair = (
        params
    )
    tok_rows = hidden.shape[0]
    local_width = attend_w.shape[2]
    gains = gain_pair.astype(jnp.float32)
    offsets = offset_pair.astype(jnp.float32)
    biases = attend_b.astype(jnp.float32)
    branches = branch_b.astype(jnp.float32)
    normed_one = layer_norm(hidden, gains[0], offsets[0]).astype(jnp.bfloat16)
    projected = jnp.dot(
        normed_one,
        attend_w.reshape(attend_w.shape[0], 3 * local_width),
        preferred_element_type=jnp.float32,
    ).reshape(tok_rows, 3, local_width)
    queries = (
        (projected[:, 0] + biases[0]).astype(jnp.bfloat16).reshape(tok_rows, head_count, HEAD_DIM)
    )
    key_now = projected[:, 1].astype(jnp.bfloat16).reshape(tok_rows, head_count, HEAD_DIM)
    value_now = (
        (projected[:, 2] + biases[1]).astype(jnp.bfloat16).reshape(tok_rows, head_count, HEAD_DIM)
    )
    key_list = [key_now]
    value_list = [value_now]
    for hop_index in range(reach_back):
        key_now, value_now = passed_along((key_now, value_now), "dp", 1)
        key_list.insert(0, key_now)
        value_list.insert(0, value_now)
    key_block = jnp.concatenate(key_list, axis=0)
    value_block = jnp.concatenate(value_list, axis=0)
    context, log_totals = attend_forward(queries, key_block, value_block, allowed)
    flat_context = context.reshape(tok_rows, local_width)
    attended = tensor_total(jnp.dot(flat_context, output_w, preferred_element_type=jnp.float32))
    middle = hidden + (attended + branches[0])
    normed_two = layer_norm(middle, gains[1], offsets[1]).astype(jnp.bfloat16)
    pre_act = jnp.dot(normed_two, expand_w, preferred_element_type=jnp.float32) + expand_b.astype(
        jnp.float32
    )
    activated = gelu_tanh(pre_act).astype(jnp.bfloat16)
    reduced = tensor_total(jnp.dot(activated, reduce_w, preferred_element_type=jnp.float32))
    output = middle + (reduced + branches[1])
    kept_state = (
        hidden,
        normed_one,
        queries,
        key_block,
        value_block,
        flat_context,
        log_totals,
        middle,
        normed_two,
        pre_act,
        activated,
    )
    return (output, kept_state)


def backward_layer(grad_out, params, kept_state, allowed, reach_back, head_count):
    attend_w, attend_b, output_w, branch_b, expand_w, expand_b, reduce_w, gain_pair, offset_pair = (
        params
    )
    (
        hidden,
        normed_one,
        queries,
        key_block,
        value_block,
        flat_context,
        log_totals,
        middle,
        normed_two,
        pre_act,
        activated,
    ) = kept_state
    tok_rows = hidden.shape[0]
    local_width = attend_w.shape[2]
    model_width = attend_w.shape[0]
    gains = gain_pair.astype(jnp.float32)
    offsets = offset_pair.astype(jnp.float32)
    bias_two = jnp.sum(grad_out, axis=0)
    grad_rounded = grad_out.astype(jnp.bfloat16)
    reduce_grad = contract("tf,td->fd", activated, grad_rounded)
    act_cot = contract("td,fd->tf", grad_rounded, reduce_w)
    unused, gelu_pull = jax.vjp(gelu_tanh, pre_act)
    pre_cot = gelu_pull(act_cot)[0]
    expand_bias_grad = jnp.sum(pre_cot, axis=0)
    pre_rounded = pre_cot.astype(jnp.bfloat16)
    expand_grad = contract("td,tf->df", normed_two, pre_rounded)
    normed_cot = input_total(contract("tf,df->td", pre_rounded, expand_w))
    unused, norm_pull = jax.vjp(layer_norm, middle, gains[1], offsets[1])
    mid_part, gain_two, offset_two = norm_pull(normed_cot)
    mid_cot = grad_out + mid_part
    bias_one = jnp.sum(mid_cot, axis=0)
    mid_rounded = mid_cot.astype(jnp.bfloat16)
    output_grad = contract("tk,td->kd", flat_context, mid_rounded)
    context_cot = (
        contract("td,kd->tk", mid_rounded, output_w)
        .astype(jnp.bfloat16)
        .reshape(tok_rows, head_count, HEAD_DIM)
    )
    query_cot, key_cot, value_cot = attend_backward(
        queries, key_block, value_block, log_totals, context_cot, allowed
    )
    key_acc = key_cot[:tok_rows]
    value_acc = value_cot[:tok_rows]
    for hop_index in range(reach_back):
        key_acc, value_acc = (
            passed_along(key_acc.astype(jnp.bfloat16), "dp", -1).astype(key_acc.dtype),
            passed_along(value_acc.astype(jnp.bfloat16), "dp", -1).astype(value_acc.dtype),
        )
        key_acc = key_acc + key_cot[(hop_index + 1) * tok_rows : (hop_index + 2) * tok_rows]
        value_acc = value_acc + value_cot[(hop_index + 1) * tok_rows : (hop_index + 2) * tok_rows]
    proj_cot = jnp.stack(
        [
            query_cot.reshape(tok_rows, local_width),
            key_acc.reshape(tok_rows, local_width),
            value_acc.reshape(tok_rows, local_width),
        ],
        axis=1,
    )
    attend_bias_grad = jnp.stack([jnp.sum(proj_cot[:, 0], axis=0), jnp.sum(proj_cot[:, 2], axis=0)])
    proj_rounded = proj_cot.astype(jnp.bfloat16).reshape(tok_rows, 3 * local_width)
    attend_grad = contract("td,tc->dc", normed_one, proj_rounded).reshape(
        model_width, 3, local_width
    )
    normed_cot_one = input_total(
        contract("tc,dc->td", proj_rounded, attend_w.reshape(model_width, 3 * local_width))
    )
    unused, first_pull = jax.vjp(layer_norm, hidden, gains[0], offsets[0])
    hid_part, gain_one, offset_one = first_pull(normed_cot_one)
    in_cot = mid_cot + hid_part
    layer_grads = (
        attend_grad,
        attend_bias_grad,
        output_grad,
        jnp.stack([bias_one, bias_two]),
        expand_grad,
        expand_bias_grad,
        reduce_grad,
        jnp.stack([gain_one, gain_two]),
        jnp.stack([offset_one, offset_two]),
    )
    return (in_cot, layer_grads)


def local(
    hidden_in,
    doc_ids,
    attend_weight,
    attend_bias,
    output_weight,
    branch_bias,
    expand_weight,
    expand_bias,
    reduce_weight,
    norm_gain,
    norm_bias,
    out_grad,
):
    layer_count = attend_weight.shape[0]
    tok_rows = hidden_in.shape[0]
    local_width = attend_weight.shape[3]
    head_count = local_width // HEAD_DIM
    reach_back = (CTX + tok_rows - 2) // tok_rows
    own_marks = doc_ids + 1
    mark_list = [own_marks]
    current_marks = own_marks
    for hop_index in range(reach_back):
        current_marks = passed_along(current_marks, "dp", 1)
        mark_list.insert(0, current_marks)
    window_marks = jnp.concatenate(mark_list, axis=0)
    window_rows = (reach_back + 1) * tok_rows
    row_ids = jnp.arange(tok_rows, dtype=jnp.int32)[:, None]
    col_ids = jnp.arange(window_rows, dtype=jnp.int32)[None, :]
    allowed = (window_marks[None, :] == own_marks[:, None]) & (
        col_ids - reach_back * tok_rows <= row_ids
    )
    saved = []
    current = hidden_in
    for layer_index in range(layer_count):
        params = (
            lax.all_gather(attend_weight[layer_index], "dp", axis=0, tiled=True),
            lax.all_gather(attend_bias[layer_index], "dp", axis=1, tiled=True),
            lax.all_gather(output_weight[layer_index], "dp", axis=0, tiled=True),
            lax.all_gather(branch_bias[layer_index], "dp", axis=1, tiled=True),
            lax.all_gather(expand_weight[layer_index], "dp", axis=0, tiled=True),
            lax.all_gather(expand_bias[layer_index], "dp", axis=0, tiled=True),
            lax.all_gather(reduce_weight[layer_index], "dp", axis=0, tiled=True),
            lax.all_gather(norm_gain[layer_index], "dp", axis=1, tiled=True),
            lax.all_gather(norm_bias[layer_index], "dp", axis=1, tiled=True),
        )
        current, kept_state = forward_layer(current, params, allowed, reach_back, head_count)
        saved.append((params, kept_state))
    grad_now = out_grad
    grad_list = [None] * layer_count
    for layer_index in reversed(range(layer_count)):
        params, kept_state = saved[layer_index]
        params = (
            lax.all_gather(attend_weight[layer_index], "dp", axis=0, tiled=True),
            lax.all_gather(attend_bias[layer_index], "dp", axis=1, tiled=True),
            lax.all_gather(output_weight[layer_index], "dp", axis=0, tiled=True),
            lax.all_gather(branch_bias[layer_index], "dp", axis=1, tiled=True),
            lax.all_gather(expand_weight[layer_index], "dp", axis=0, tiled=True),
            lax.all_gather(expand_bias[layer_index], "dp", axis=0, tiled=True),
            lax.all_gather(reduce_weight[layer_index], "dp", axis=0, tiled=True),
            lax.all_gather(norm_gain[layer_index], "dp", axis=1, tiled=True),
            lax.all_gather(norm_bias[layer_index], "dp", axis=1, tiled=True),
        )
        grad_now, layer_grads = backward_layer(
            grad_now, params, kept_state, allowed, reach_back, head_count
        )
        grad_list[layer_index] = layer_grads
    stacked = [jnp.stack([entry[member] for entry in grad_list]) for member in range(9)]
    (
        attend_all,
        attend_bias_all,
        output_all,
        branch_all,
        expand_all,
        expand_bias_all,
        reduce_all,
        gain_all,
        offset_all,
    ) = stacked
    owned = (
        lax.psum_scatter(
            attend_all.astype(jnp.bfloat16), "dp", scatter_dimension=1, tiled=True
        ).astype(jnp.float32),
        lax.psum_scatter(
            attend_bias_all.astype(jnp.bfloat16), "dp", scatter_dimension=2, tiled=True
        ).astype(jnp.float32),
        lax.psum_scatter(
            output_all.astype(jnp.bfloat16), "dp", scatter_dimension=1, tiled=True
        ).astype(jnp.float32),
        lax.psum_scatter(
            branch_all.astype(jnp.bfloat16), "dp", scatter_dimension=2, tiled=True
        ).astype(jnp.float32),
        lax.psum_scatter(
            expand_all.astype(jnp.bfloat16), "dp", scatter_dimension=1, tiled=True
        ).astype(jnp.float32),
        lax.psum_scatter(
            expand_bias_all.astype(jnp.bfloat16), "dp", scatter_dimension=1, tiled=True
        ).astype(jnp.float32),
        lax.psum_scatter(
            reduce_all.astype(jnp.bfloat16), "dp", scatter_dimension=1, tiled=True
        ).astype(jnp.float32),
        lax.psum_scatter(
            gain_all.astype(jnp.bfloat16), "dp", scatter_dimension=2, tiled=True
        ).astype(jnp.float32),
        lax.psum_scatter(
            offset_all.astype(jnp.bfloat16), "dp", scatter_dimension=2, tiled=True
        ).astype(jnp.float32),
    )
    return (
        current,
        grad_now,
        owned[0],
        owned[1],
        owned[2],
        owned[3],
        owned[4],
        owned[5],
        owned[6],
        owned[7],
        owned[8],
    )


def solution(mesh):
    return jax.shard_map(
        local,
        mesh=mesh,
        in_specs=(
            P("dp", None),
            P("dp"),
            P(None, "dp", None, "tensor"),
            P(None, None, ("tensor", "dp")),
            P(None, ("tensor", "dp"), None),
            P(None, None, "dp"),
            P(None, "dp", "tensor"),
            P(None, ("tensor", "dp")),
            P(None, ("tensor", "dp"), None),
            P(None, None, "dp"),
            P(None, None, "dp"),
            P("dp", None),
        ),
        out_specs=(
            P("dp", None),
            P("dp", None),
            P(None, "dp", None, "tensor"),
            P(None, None, ("tensor", "dp")),
            P(None, ("tensor", "dp"), None),
            P(None, None, "dp"),
            P(None, "dp", "tensor"),
            P(None, ("tensor", "dp")),
            P(None, ("tensor", "dp"), None),
            P(None, None, "dp"),
            P(None, None, "dp"),
        ),
        check_vma=False,
    )
```

profile of v0, /device:TPU:0, one launch (start us, length us, event | category | flops | bytes accessed | tf_op | source)
XLA Modules:
  0.0 1307.2 jit_solution(5667303373786951555)
XLA Ops:
  13.1 10.3 all-gather.3
  25.4 8.8 all-gather.1
  46.6 9.9 all-gather.4
  92.4 12.5 all-gather.7
  112.5 33.4 %all-reduce.9.cloned.1.call-done = bf16[512,1024]{1,0:T(8,128)(2,1)} async-done(((bf16[512,1024]{1,0:T(8,128)(2,1)}), bf16[512,1024]{1,0:T(8,128)(2,1)}) %all-reduce.9.cloned.1.call-update) | async-done | bytes 1048592 | tf_op jit(solution)/shard_map/psum | solution.py:61
  148.5 27.0 %all-gather.27.cloned.1.call-done = bf16[1,1024,1024]{2,1,0:T(8,128)(2,1)} async-done(((bf16[1,128,1024]{2,1,0:T(8,128)(2,1)}), bf16[1,1024,1024]{2,1,0:T(8,128)(2,1)}) %all-gather.27.cloned.1.call-update) | async-done | bytes 2097168 | tf_op jit(solution)/shard_map/all_gather | solution.py:254
  179.7 25.3 %all-gather.29.cloned.1.call-done = bf16[1,1024,1024]{2,1,0:T(8,128)(2,1)} async-done(((bf16[1,128,1024]{2,1,0:T(8,128)(2,1)}), bf16[1,1024,1024]{2,1,0:T(8,128)(2,1)}) %all-gather.29.cloned.1.call-update) | async-done | bytes 2097168 | tf_op jit(solution)/shard_map/all_gather | solution.py:256
  209.9 9.5 all-gather.12
  231.3 8.6 all-gather.9
  242.6 44.7 %all-reduce.11.cloned.1.call-done = bf16[512,1024]{1,0:T(8,128)(2,1)} async-done(((bf16[512,1024]{1,0:T(8,128)(2,1)}), bf16[512,1024]{1,0:T(8,128)(2,1)}) %all-reduce.11.cloned.1.call-update) | async-done | bytes 1048592 | tf_op jit(solution)/shard_map/psum | solution.py:61
  301.8 13.4 %all-gather.13 = bf16[1,256,1024]{2,1,0:T(8,128)(2,1)S(1)} all-gather(bf16[1,32,1024]{2,1,0:T(8,128)(2,1)S(1)} %get-tuple-element.52), channel_id=15, replica_groups=mesh['dp'=8,'tensor'=4] {'dp'}, dimensions={1}, use_global_device_ids=true | all-gather | bytes 589824 | tf_op jit(solution)/shard_map/all_gather | solution.py:252
  330.3 8.8 all-gather.16
  339.1 8.4 all-gather.14
  347.5 32.1 %all-reduce.13.cloned.1.call-done = bf16[512,1024]{1,0:T(8,128)(2,1)} async-done(((bf16[512,1024]{1,0:T(8,128)(2,1)}), bf16[512,1024]{1,0:T(8,128)(2,1)}) %all-reduce.13.cloned.1.call-update) | async-done | bytes 1048592 | tf_op jit(solution)/shard_map/psum | solution.py:61
  382.8 26.3 %all-gather.33.cloned.1.call-done = bf16[1,1024,1024]{2,1,0:T(8,128)(2,1)} async-done(((bf16[1,128,1024]{2,1,0:T(8,128)(2,1)}), bf16[1,1024,1024]{2,1,0:T(8,128)(2,1)}) %all-gather.33.cloned.1.call-update) | async-done | bytes 2097168 | tf_op jit(solution)/shard_map/all_gather | solution.py:254
  414.0 24.8 %all-gather.35.cloned.1.call-done = bf16[1,1024,1024]{2,1,0:T(8,128)(2,1)} async-done(((bf16[1,128,1024]{2,1,0:T(8,128)(2,1)}), bf16[1,1024,1024]{2,1,0:T(8,128)(2,1)}) %all-gather.35.cloned.1.call-update) | async-done | bytes 2097168 | tf_op jit(solution)/shard_map/all_gather | solution.py:256
  448.0 52.0 %all-reduce.15.cloned.1.call-done = bf16[512,1024]{1,0:T(8,128)(2,1)} async-done(((bf16[512,1024]{1,0:T(8,128)(2,1)}), bf16[512,1024]{1,0:T(8,128)(2,1)}) %all-reduce.15.cloned.1.call-update) | async-done | bytes 1048592 | tf_op jit(solution)/shard_map/psum | solution.py:65
  524.3 30.5 %fusion.42 = f32[1536,4,64]{0,2,1:T(8,128)} fusion(f32[4,512,1536]{2,1,0:T(8,128)} %fusion.140, f32[4,512,1536]{2,1,0:T(8,128)} %copy-done.76, f32[4,512]{1,0:T(4,128)S(1)} %log.14, pred[512,1536]{1,0:T(8,128)(4,1)} %copy-done.38, f32[512,4,64]{0,2,1:T(8,128)} %bitcast.218, f32[4,64]{1,0:T(4,128)S(1)} %add.331), kind=kOutput, calls=%fused_computation.50 | convolution fusion | flops 437521920 | bytes 28058624 | tf_op jit(solution)/shard_map/hqk,qhe->khe/dot_general | solution.py:19
  563.5 26.2 %bitcast_reduce_fusion.1 = (bf16[4,64]{1,0:T(4,128)(2,1)S(1)}, bf16[4,64,512]{2,1,0:T(8,128)(2,1)}) fusion(f32[4,512,1536]{2,1,0:T(8,128)} %fusion.140, f32[4,512]{1,0:T(4,128)S(1)} %log.14, f32[4,512,1536]{2,1,0:T(8,128)} %copy-done.76, pred[512,1536]{1,0:T(8,128)(4,1)} %copy-done.38, bf16[512,4,64]{0,2,1:T(8,128)(2,1)} %bitcast.224, ...), kind=kOutput, calls=%fused_computation.179 | convolution fusion | flops 439880960 | bytes 27009536 | tf_op jit(solution)/shard_map/hqk,khe->qhe/dot_general | solution.py:19
  602.7 57.1 %all-reduce.17.cloned.1.call-done = bf16[512,1024]{1,0:T(8,128)(2,1)} async-done(((bf16[512,1024]{1,0:T(8,128)(2,1)}), bf16[512,1024]{1,0:T(8,128)(2,1)}) %all-reduce.17.cloned.1.call-update) | async-done | bytes 1048592 | tf_op jit(solution)/shard_map/psum | solution.py:65
  672.4 51.2 %all-reduce.19.cloned.1.call-done = bf16[512,1024]{1,0:T(8,128)(2,1)} async-done(((bf16[512,1024]{1,0:T(8,128)(2,1)}), bf16[512,1024]{1,0:T(8,128)(2,1)}) %all-reduce.19.cloned.1.call-update) | async-done | bytes 1048592 | tf_op jit(solution)/shard_map/psum | solution.py:65
  746.8 31.0 %fusion.39 = f32[1536,4,64]{0,2,1:T(8,128)} fusion(f32[4,512,1536]{2,1,0:T(8,128)} %fusion.142, f32[4,512,1536]{2,1,0:T(8,128)} %copy-done.75, f32[4,512]{1,0:T(4,128)S(1)} %log.15, pred[512,1536]{1,0:T(8,128)(4,1)} %copy-done.38, f32[512,4,64]{0,2,1:T(8,128)} %bitcast.216, f32[4,64]{1,0:T(4,128)S(1)} %add.305), kind=kOutput, calls=%fused_computation.49 | convolution fusion | flops 437521920 | bytes 28058624 | tf_op jit(solution)/shard_map/hqk,qhe->khe/dot_general | solution.py:19
  791.2 26.0 %bitcast_reduce_fusion = (bf16[4,64]{1,0:T(4,128)(2,1)S(1)}, bf16[4,64,512]{2,1,0:T(8,128)(2,1)}) fusion(f32[4,512,1536]{2,1,0:T(8,128)} %fusion.142, f32[4,512]{1,0:T(4,128)S(1)} %log.15, f32[4,512,1536]{2,1,0:T(8,128)} %copy-done.75, pred[512,1536]{1,0:T(8,128)(4,1)} %copy-done.38, bf16[512,4,64]{0,2,1:T(8,128)(2,1)S(1)} %bitcast.221, ...), kind=kOutput, calls=%fused_computation.178 | convolution fusion | flops 439880960 | bytes 27009536 | tf_op jit(solution)/shard_map/hqk,khe->qhe/dot_general | solution.py:19
  853.2 65.1 %all-reduce.21.cloned.1.call-done = (bf16[512,1024]{1,0:T(8,128)(2,1)}, bf16[512,1024]{1,0:T(8,128)(2,1)}) async-done(((bf16[512,1024]{1,0:T(8,128)(2,1)}, bf16[512,1024]{1,0:T(8,128)(2,1)}), (bf16[512,1024]{1,0:T(8,128)(2,1)}, bf16[512,1024]{1,0:T(8,128)(2,1)})) %all-reduce.21.cloned.1.call-update) | async-done | bytes 2097168 | tf_op jit(solution)/shard_map/psum | solution.py:61
  961.2 29.3 %reduce-scatter.30.cloned.1.call-done = bf16[128,4]{1,0:T(8,128)(2,1)} async-done(((bf16[1024,4]{1,0:T(8,128)(2,1)}), bf16[128,4]{1,0:T(8,128)(2,1)}) %reduce-scatter.30.cloned.1.call-update) | async-done | bytes 1040
  992.1 34.9 %reduce-scatter.28.cloned.1.call-done = bf16[32,4]{1,0:T(8,128)(2,1)} async-done(((bf16[256,4]{1,0:T(8,128)(2,1)}), bf16[32,4]{1,0:T(8,128)(2,1)}) %reduce-scatter.28.cloned.1.call-update) | async-done | bytes 272
  1028.4 37.6 %reduce-scatter.22.cloned.1.call-done = bf16[2,32,1024]{2,1,0:T(8,128)(2,1)} async-done(((bf16[2,256,1024]{2,1,0:T(8,128)(2,1)}), bf16[2,32,1024]{2,1,0:T(8,128)(2,1)}) %reduce-scatter.22.cloned.1.call-update) | async-done | bytes 131088 | tf_op jit(solution)/shard_map/reduce_scatter | solution.py:300
  1072.8 30.3 %reduce-scatter.34.cloned.1.call-done = bf16[128,4]{1,0:T(8,128)(2,1)} async-done(((bf16[1024,4]{1,0:T(8,128)(2,1)}), bf16[128,4]{1,0:T(8,128)(2,1)}) %reduce-scatter.34.cloned.1.call-update) | async-done | bytes 1040
  1104.7 35.2 %reduce-scatter.36.cloned.1.call-done = bf16[128,4]{1,0:T(8,128)(2,1)} async-done(((bf16[1024,4]{1,0:T(8,128)(2,1)}), bf16[128,4]{1,0:T(8,128)(2,1)}) %reduce-scatter.36.cloned.1.call-update) | async-done | bytes 1040
  1141.4 52.8 %reduce-scatter.24.cloned.1.call-done = bf16[2,128,1024]{2,1,0:T(8,128)(2,1)} async-done(((bf16[2,1024,1024]{2,1,0:T(8,128)(2,1)}), bf16[2,128,1024]{2,1,0:T(8,128)(2,1)}) %reduce-scatter.24.cloned.1.call-update) | async-done | bytes 524304 | tf_op jit(solution)/shard_map/reduce_scatter | solution.py:306
  1196.4 52.4 %reduce-scatter.26.cloned.1.call-done = bf16[2,128,1024]{2,1,0:T(8,128)(2,1)} async-done(((bf16[2,1024,1024]{2,1,0:T(8,128)(2,1)}), bf16[2,128,1024]{2,1,0:T(8,128)(2,1)}) %reduce-scatter.26.cloned.1.call-update) | async-done | bytes 524304 | tf_op jit(solution)/shard_map/reduce_scatter | solution.py:312
  1250.9 47.3 %reduce-scatter.20.cloned.1.call-done = bf16[2,128,3,256]{3,1,2,0:T(8,128)(2,1)} async-done(((bf16[2,1024,3,256]{3,1,2,0:T(8,128)(2,1)}), bf16[2,128,3,256]{3,1,2,0:T(8,128)(2,1)}) %reduce-scatter.20.cloned.1.call-update) | async-done | bytes 393232 | tf_op jit(solution)/shard_map/reduce_scatter | solution.py:294
  (441 shorter events, 328.7 us)
Async XLA Ops:
  7.2 52.3 %all-gather.25.cloned.1.call-start = ((), (), s32[]{:S(2)}) async-start(), calls=%async_computation.19 | async-start | bytes 1769472 | tf_op jit(solution)/shard_map/all_gather | solution.py:250
  9.2 136.7 %all-reduce.9.cloned.1.call-start = ((), (), s32[]{:S(2)}) async-start(), calls=%async_computation.9 | async-start | bytes 2097152 | tf_op jit(solution)/shard_map/psum | solution.py:61
  9.9 46.5 %collective-permute-start.2 = (s32[512]{0:T(512)S(1)}, s32[512]{0:T(512)S(1)}, u32[]{:S(2)}, u32[]{:S(2)}) collective-permute-start(s32[512]{0:T(512)S(1)} %broadcast_add_fusion), channel_id=1, source_target_pairs={{0,4},{4,8},{8,12},{12,16},{16,20},{20,24},{24,28},{1,5},{5,9},{9,... | collective-permute-start | bytes 6152 | tf_op jit(solution)/shard_map/ppermute | solution.py:15
  89.9 85.6 %all-gather.27.cloned.1.call-start = ((), (), s32[]{:S(2)}) async-start(), calls=%async_computation.20 | async-start | bytes 2359296 | tf_op jit(solution)/shard_map/all_gather | solution.py:254
  90.8 114.2 %all-gather.29.cloned.1.call-start = ((), (), s32[]{:S(2)}) async-start(), calls=%async_computation.21 | async-start | bytes 2359296 | tf_op jit(solution)/shard_map/all_gather | solution.py:256
  91.7 148.2 %all-gather.31.cloned.1.call-start = ((), (), s32[]{:S(2)}) async-start(), calls=%async_computation.22 | async-start | bytes 1769472 | tf_op jit(solution)/shard_map/all_gather | solution.py:250
  92.3 195.0 %all-reduce.11.cloned.1.call-start = ((), (), s32[]{:S(2)}) async-start(), calls=%async_computation.10 | async-start | bytes 2097152 | tf_op jit(solution)/shard_map/psum | solution.py:61
  209.7 169.8 %all-reduce.13.cloned.1.call-start = ((), (), s32[]{:S(2)}) async-start(), calls=%async_computation.11 | async-start | bytes 2097152 | tf_op jit(solution)/shard_map/psum | solution.py:61
  295.8 19.3 %collective-permute-start.6 = (bf16[512,4,64]{0,2,1:T(8,128)(2,1)S(1)}, bf16[512,4,64]{0,2,1:T(8,128)(2,1)}, u32[]{:S(2)}, u32[]{:S(2)}) collective-permute-start(bf16[512,4,64]{0,2,1:T(8,128)(2,1)S(1)} %add_convert_fusion.5), channel_id=1, source_target_pairs={{0,4},{4,8},{8,12},{12,16},{16,20},{20,24},{24,28},{1,5},{5,9},{9,... | collective-permute-start | bytes 786440 | tf_op jit(solution)/shard_map/ppermute | solution.py:15
  299.4 18.0 %collective-permute-start.9 = (bf16[512,4,64]{0,2,1:T(8,128)(2,1)}, bf16[512,4,64]{0,2,1:T(8,128)(2,1)}, u32[]{:S(2)}, u32[]{:S(2)}) collective-permute-start(bf16[512,4,64]{0,2,1:T(8,128)(2,1)} %collective-permute-done.8), channel_id=1, source_target_pairs={{0,4},{4,8},{8,12},{12,16},{16,20},{20,24},{24,28},{1,5},{5,9},{9,... | collective-permute-start | bytes 786440 | tf_op jit(solution)/shard_map/ppermute | solution.py:15
  328.7 80.4 %all-gather.33.cloned.1.call-start = ((), (), s32[]{:S(2)}) async-start(), calls=%async_computation.23 | async-start | bytes 2359296 | tf_op jit(solution)/shard_map/all_gather | solution.py:254
  329.5 109.3 %all-gather.35.cloned.1.call-start = ((), (), s32[]{:S(2)}) async-start(), calls=%async_computation.24 | async-start | bytes 2359296 | tf_op jit(solution)/shard_map/all_gather | solution.py:256
  330.2 169.7 %all-reduce.15.cloned.1.call-start = ((), (), s32[]{:S(2)}) async-start(), calls=%async_computation.12 | async-start | bytes 2097152 | tf_op jit(solution)/shard_map/psum | solution.py:65
  447.9 211.9 %all-reduce.17.cloned.1.call-start = ((), (), s32[]{:S(2)}) async-start(), calls=%async_computation.13 | async-start | bytes 2097152 | tf_op jit(solution)/shard_map/psum | solution.py:65
  515.2 41.9 %collective-permute-start.12 = (bf16[512,4,64]{0,2,1:T(8,128)(2,1)}, bf16[512,4,64]{0,2,1:T(8,128)(2,1)}, u32[]{:S(2)}, u32[]{:S(2)}) collective-permute-start(bf16[512,4,64]{0,2,1:T(8,128)(2,1)} %slice.306), channel_id=1, source_target_pairs={{4,0},{8,4},{12,8},{16,12},{20,16},{24,20},{28,24},{5,1},{9,5},{13... | collective-permute-start | bytes 786440 | tf_op jit(solution)/shard_map/ppermute | solution.py:15
  559.1 32.4 %collective-permute-start.13 = (bf16[512,4,64]{0,2,1:T(8,128)(2,1)}, bf16[512,4,64]{0,2,1:T(8,128)(2,1)}, u32[]{:S(2)}, u32[]{:S(2)}) collective-permute-start(bf16[512,4,64]{0,2,1:T(8,128)(2,1)} %fusion.121), channel_id=1, source_target_pairs={{4,0},{8,4},{12,8},{16,12},{20,16},{24,20},{28,24},{5,1},{9,5},{13... | collective-permute-start | bytes 786440 | tf_op jit(solution)/shard_map/ppermute | solution.py:15
  562.2 33.0 %collective-permute-start.11 = (bf16[512,4,64]{0,2,1:T(8,128)(2,1)}, bf16[512,4,64]{0,2,1:T(8,128)(2,1)}, u32[]{:S(2)}, u32[]{:S(2)}) collective-permute-start(bf16[512,4,64]{0,2,1:T(8,128)(2,1)} %fusion.122), channel_id=1, source_target_pairs={{4,0},{8,4},{12,8},{16,12},{20,16},{24,20},{28,24},{5,1},{9,5},{13... | collective-permute-start | bytes 786440 | tf_op jit(solution)/shard_map/ppermute | solution.py:15
  602.5 121.2 %all-reduce.19.cloned.1.call-start = ((), (), s32[]{:S(2)}) async-start(), calls=%async_computation.14 | async-start | bytes 2097152 | tf_op jit(solution)/shard_map/psum | solution.py:65
  672.4 246.0 %all-reduce.21.cloned.1.call-start = ((), (), s32[]{:S(2)}) async-start(), calls=%async_computation.30 | async-start | bytes 4194304 | tf_op jit(solution)/shard_map/psum | solution.py:61
  738.9 45.9 %collective-permute-start.16 = (bf16[512,4,64]{0,2,1:T(8,128)(2,1)}, bf16[512,4,64]{0,2,1:T(8,128)(2,1)}, u32[]{:S(2)}, u32[]{:S(2)}) collective-permute-start(bf16[512,4,64]{0,2,1:T(8,128)(2,1)} %slice.304), channel_id=1, source_target_pairs={{4,0},{8,4},{12,8},{16,12},{20,16},{24,20},{28,24},{5,1},{9,5},{13... | collective-permute-start | bytes 786440 | tf_op jit(solution)/shard_map/ppermute | solution.py:15
  778.8 9.2 collective-permute-start.14
  786.8 32.2 %collective-permute-start.17 = (bf16[512,4,64]{0,2,1:T(8,128)(2,1)}, bf16[512,4,64]{0,2,1:T(8,128)(2,1)}, u32[]{:S(2)}, u32[]{:S(2)}) collective-permute-start(bf16[512,4,64]{0,2,1:T(8,128)(2,1)} %fusion.119), channel_id=1, source_target_pairs={{4,0},{8,4},{12,8},{16,12},{20,16},{24,20},{28,24},{5,1},{9,5},{13... | collective-permute-start | bytes 786440 | tf_op jit(solution)/shard_map/ppermute | solution.py:15
  789.9 31.2 %collective-permute-start.15 = (bf16[512,4,64]{0,2,1:T(8,128)(2,1)}, bf16[512,4,64]{0,2,1:T(8,128)(2,1)}, u32[]{:S(2)}, u32[]{:S(2)}) collective-permute-start(bf16[512,4,64]{0,2,1:T(8,128)(2,1)} %fusion.120), channel_id=1, source_target_pairs={{4,0},{8,4},{12,8},{16,12},{20,16},{24,20},{28,24},{5,1},{9,5},{13... | collective-permute-start | bytes 786440 | tf_op jit(solution)/shard_map/ppermute | solution.py:15
  827.7 131.9 %reduce-scatter.32.cloned.1.call-start = ((), (), s32[]{:S(2)}) async-start(), calls=%async_computation.27 | async-start | bytes 294912
  832.3 158.3 %reduce-scatter.30.cloned.1.call-start = ((), (), s32[]{:S(2)}) async-start(), calls=%async_computation.26 | async-start | bytes 294912
  838.6 188.4 %reduce-scatter.28.cloned.1.call-start = ((), (), s32[]{:S(2)}) async-start(), calls=%async_computation.25 | async-start | bytes 73728
  839.7 226.3 %reduce-scatter.22.cloned.1.call-start = ((), (), s32[]{:S(2)}) async-start(), calls=%async_computation.16 | async-start | bytes 1179648 | tf_op jit(solution)/shard_map/reduce_scatter | solution.py:300
  842.0 261.2 %reduce-scatter.34.cloned.1.call-start = ((), (), s32[]{:S(2)}) async-start(), calls=%async_computation.28 | async-start | bytes 294912
  926.9 213.0 %reduce-scatter.36.cloned.1.call-start = ((), (), s32[]{:S(2)}) async-start(), calls=%async_computation.29 | async-start | bytes 294912
  930.2 264.0 %reduce-scatter.24.cloned.1.call-start = ((), (), s32[]{:S(2)}) async-start(), calls=%async_computation.17 | async-start | bytes 4718592 | tf_op jit(solution)/shard_map/reduce_scatter | solution.py:306
  934.9 313.9 %reduce-scatter.26.cloned.1.call-start = ((), (), s32[]{:S(2)}) async-start(), calls=%async_computation.18 | async-start | bytes 4718592 | tf_op jit(solution)/shard_map/reduce_scatter | solution.py:312
  943.1 355.2 %reduce-scatter.20.cloned.1.call-start = ((), (), s32[]{:S(2)}) async-start(), calls=%async_computation.15 | async-start | bytes 3538944 | tf_op jit(solution)/shard_map/reduce_scatter | solution.py:294
  (89 other events, 934.7 us)
Sparse Core Ops, SparseCore 0:
  10.5 28.3 all-gather.24
  90.0 55.8 all-reduce.8
  148.4 27.0 all-gather.26
  177.2 27.7 all-gather.28
  206.8 25.7 all-gather.30
  235.3 51.8 all-reduce.10
  328.9 50.6 all-reduce.12
  382.0 27.0 all-gather.32
  411.0 27.7 all-gather.34
  448.1 51.8 all-reduce.14
  602.6 57.1 all-reduce.16
  672.5 51.1 all-reduce.18
  827.8 90.4 all-reduce.20
  921.2 32.6 reduce-scatter.31
  956.8 33.6 reduce-scatter.29
  993.4 33.5 reduce-scatter.27
  1030.0 35.9 reduce-scatter.21
  1069.5 33.6 reduce-scatter.33
  1106.2 33.6 reduce-scatter.35
  1143.1 51.0 reduce-scatter.23
  1197.6 51.0 reduce-scatter.25
  1252.1 46.0 reduce-scatter.19
where the time goes:
time: 1320 us; the launch traced here: 1310 us
  waiting for transfers between devices  762 us (58%)
  matrix products  231 us (18%)
  blocking collectives  114 us (9%)
  other arithmetic  75.3 us (6%)
  local copies, waits for them, and re-layouts  67.7 us (5%)
  starting transfers between devices  42.3 us (3%)
  between operations  16 us (1%)
    dot_general x28, matrix products, contract(): jnp.einsum(pattern, left_side, right_side, preferred_element_type=jnp.flo...  206 us
    psum x4, waiting for transfers between devices, tensor_total(): lax.psum(partial_value.astype(jnp.bfloat16), 'tensor').astype(jnp.float32)  175 us
    psum x3, waiting for transfers between devices, input_total(): lax.psum(partial_value.astype(jnp.bfloat16), 'tensor').astype(jnp.float32)  160 us
    unnamed x27, waiting for transfers between devices  132 us
    all_gather x2, waiting for transfers between devices, local(): lax.all_gather(expand_weight[layer_index], 'dp', axis=0, tiled=True)  53.3 us
    reduce_scatter x1, waiting for transfers between devices, local(): lax.psum_scatter(expand_all.astype(jnp.bfloat16), 'dp', scatter_dimension...  52.8 us
    reduce_scatter x1, waiting for transfers between devices, local(): lax.psum_scatter(reduce_all.astype(jnp.bfloat16), 'dp', scatter_dimension...  52.4 us
    all_gather x2, waiting for transfers between devices, local(): lax.all_gather(reduce_weight[layer_index], 'dp', axis=0, tiled=True)  50.1 us
  transfers between devices with their start and end apart: 40, of which 20 were waited for; matrix products, arithmetic and copies ran while one was open for 21% of the time, Pallas kernels for 0%

commit v1 on v0

v1 whole, which is shorter than its diff:
```python
import functools
import math

import jax
import jax.numpy as jnp
from jax import lax
from jax.experimental import pallas as pl
from jax.experimental.pallas import tpu as pltpu
from jax.sharding import PartitionSpec as P

HEAD_DIM = 64
CTX = 1024
LANES = 128
ROW_TILE = 256


def passed_along(block, axis, distance):
    devices = range(lax.axis_size(axis))
    route = [(i - distance, i) for i in devices if i - distance in devices]
    return lax.ppermute(block, axis, route)


def contract(pattern, left_side, right_side):
    return jnp.einsum(pattern, left_side, right_side, preferred_element_type=jnp.float32)


def layer_norm(values, gain_row, offset_row):
    center = values - jnp.mean(values, axis=-1, keepdims=True)
    spread = jnp.mean(center * center, axis=-1, keepdims=True)
    return center * lax.rsqrt(spread + 1e-05) * gain_row + offset_row


def gelu_tanh(values):
    return (
        0.5
        * values
        * (1.0 + jnp.tanh(0.7978845608028654 * (values + 0.044715 * values * values * values)))
    )


def dot_rows(left_side, right_side):
    return lax.dot_general(
        left_side, right_side, (((1,), (1,)), ((), ())), preferred_element_type=jnp.float32
    )


def dot_tokens(left_side, right_side):
    return lax.dot_general(
        left_side, right_side, (((0,), (0,)), ((), ())), preferred_element_type=jnp.float32
    )


def row_tiles(rows, window_rows):
    tile = min(ROW_TILE, rows)
    back = window_rows - rows
    for start in range(0, rows, tile):
        low = max(0, (back + start - CTX + 1) // LANES * LANES)
        yield start, tile, low, back + start + tile


def tile_mask(own_ref, window_ref, start, tile, low, high, back):
    own = own_ref[start : start + tile, :]
    window = window_ref[:, low:high]
    row = lax.broadcasted_iota(jnp.int32, (tile, high - low), 0) + (start + back)
    col = lax.broadcasted_iota(jnp.int32, (tile, high - low), 1) + low
    return (window == own) & (col <= row)


def head_parts(width):
    group = min(LANES, width)
    for base in range(0, width, group):
        for inner in range(0, group, HEAD_DIM):
            yield base, group, inner


def pick(block, inner):
    lane = lax.broadcasted_iota(jnp.int32, block.shape, 1)
    return jnp.where((lane >= inner) & (lane < inner + HEAD_DIM), block, jnp.zeros_like(block))


def forward_kernel(q_ref, kv_ref, own_ref, window_ref, o_ref, lse_ref):
    rows, width = q_ref.shape
    window_rows = kv_ref.shape[0]
    back = window_rows - rows
    factor = 1.0 / math.sqrt(HEAD_DIM)
    for start, tile, low, high in row_tiles(rows, window_rows):
        allowed = tile_mask(own_ref, window_ref, start, tile, low, high, back)
        held = None
        logs = []
        for base, group, inner in head_parts(width):
            queries = pick(q_ref[start : start + tile, base : base + group], inner)
            keys = kv_ref[low:high, base : base + group]
            values = kv_ref[low:high, width + base : width + base + group]
            unnormed = jnp.where(allowed, jnp.exp(dot_rows(queries, keys) * factor), 0.0)
            totals = jnp.sum(unnormed, axis=-1, keepdims=True)
            probabilities = (unnormed * (1.0 / totals)).astype(jnp.bfloat16)
            context = pick(
                jnp.dot(probabilities, values, preferred_element_type=jnp.float32), inner
            )
            held = context if inner == 0 else held + context
            logs.append(jnp.log(totals))
            if inner + HEAD_DIM == group:
                o_ref[start : start + tile, base : base + group] = held.astype(jnp.bfloat16)
        for index, entry in enumerate(logs):
            lse_ref[start : start + tile, index : index + 1] = entry


def backward_kernel(
    q_ref, kv_ref, lse_ref, cot_ref, own_ref, window_ref, dq_ref, own_out, back_out, acc
):
    rows, width = q_ref.shape
    window_rows = kv_ref.shape[0]
    back = window_rows - rows
    factor = 1.0 / math.sqrt(HEAD_DIM)
    acc[...] = jnp.zeros_like(acc)
    for start, tile, low, high in row_tiles(rows, window_rows):
        allowed = tile_mask(own_ref, window_ref, start, tile, low, high, back)
        held = None
        for index, (base, group, inner) in enumerate(head_parts(width)):
            queries = pick(q_ref[start : start + tile, base : base + group], inner)
            cots = pick(cot_ref[start : start + tile, base : base + group], inner)
            keys = kv_ref[low:high, base : base + group]
            values = kv_ref[low:high, width + base : width + base + group]
            logs = lse_ref[start : start + tile, index : index + 1]
            scores = dot_rows(queries, keys) * factor
            probabilities = jnp.where(allowed, jnp.exp(scores - logs), 0.0)
            rounded = probabilities.astype(jnp.bfloat16)
            acc[low:high, width + base : width + base + group] += dot_tokens(rounded, cots)
            prob_cot = dot_rows(cots, values)
            inner_sum = jnp.sum(probabilities * prob_cot, axis=-1, keepdims=True)
            score_cot = (probabilities * (prob_cot - inner_sum) * factor).astype(jnp.bfloat16)
            acc[low:high, base : base + group] += dot_tokens(score_cot, queries)
            part = pick(jnp.dot(score_cot, keys, preferred_element_type=jnp.float32), inner)
            held = part if inner == 0 else held + part
            if inner + HEAD_DIM == group:
                dq_ref[start : start + tile, base : base + group] = held
    own_out[...] = acc[back:, :]
    back_out[...] = acc[:back, :].astype(jnp.bfloat16)


def in_vmem(count):
    return [pl.BlockSpec(memory_space=pltpu.VMEM)] * count


def attend_forward(queries, window_kv, own_marks, window_marks):
    rows, width = queries.shape
    return pl.pallas_call(
        forward_kernel,
        out_shape=(
            jax.ShapeDtypeStruct((rows, width), jnp.bfloat16),
            jax.ShapeDtypeStruct((rows, width // HEAD_DIM), jnp.float32),
        ),
        in_specs=in_vmem(4),
        out_specs=tuple(in_vmem(2)),
        compiler_params=pltpu.CompilerParams(vmem_limit_bytes=40 * 1024 * 1024),
        name="attend_forward",
    )(queries, window_kv, own_marks, window_marks)


def attend_backward(queries, window_kv, log_totals, out_cot, own_marks, window_marks):
    rows, width = queries.shape
    window_rows = window_kv.shape[0]
    return pl.pallas_call(
        backward_kernel,
        out_shape=(
            jax.ShapeDtypeStruct((rows, width), jnp.float32),
            jax.ShapeDtypeStruct((rows, 2 * width), jnp.float32),
            jax.ShapeDtypeStruct((window_rows - rows, 2 * width), jnp.bfloat16),
        ),
        in_specs=in_vmem(6),
        out_specs=tuple(in_vmem(3)),
        scratch_shapes=[pltpu.VMEM((window_rows, 2 * width), jnp.float32)],
        compiler_params=pltpu.CompilerParams(vmem_limit_bytes=48 * 1024 * 1024),
        name="attend_backward",
    )(queries, window_kv, log_totals, out_cot, own_marks, window_marks)


def tensor_total(partial_value):
    return lax.psum(partial_value.astype(jnp.bfloat16), "tensor").astype(jnp.float32)


def forward_layer(hidden, params, marks, reach_back):
    attend_w, attend_b, output_w, branches, expand_w, expand_b, reduce_w, gains, offsets = params
    width = output_w.shape[0]
    own_marks, window_marks = marks
    normed_one = layer_norm(hidden, gains[0], offsets[0]).astype(jnp.bfloat16)
    projected = jnp.dot(normed_one, attend_w, preferred_element_type=jnp.float32)
    queries = (projected[:, :width] + attend_b[0]).astype(jnp.bfloat16)
    kv_bias = jnp.concatenate([jnp.zeros_like(attend_b[1]), attend_b[1]])
    kv_now = (projected[:, width:] + kv_bias).astype(jnp.bfloat16)
    kv_list = [passed_along(kv_now, "dp", hop) for hop in range(reach_back, 0, -1)]
    window_kv = jnp.concatenate(kv_list + [kv_now], axis=0)
    context, log_totals = attend_forward(queries, window_kv, own_marks, window_marks)
    attended = tensor_total(jnp.dot(context, output_w, preferred_element_type=jnp.float32))
    middle = hidden + (attended + branches[0])
    normed_two = layer_norm(middle, gains[1], offsets[1]).astype(jnp.bfloat16)
    pre_act = jnp.dot(normed_two, expand_w, preferred_element_type=jnp.float32) + expand_b
    activated = gelu_tanh(pre_act).astype(jnp.bfloat16)
    reduced = tensor_total(jnp.dot(activated, reduce_w, preferred_element_type=jnp.float32))
    output = middle + (reduced + branches[1])
    kept_state = (
        hidden,
        normed_one,
        queries,
        window_kv,
        context,
        log_totals,
        middle,
        normed_two,
        pre_act,
        activated,
    )
    return (output, kept_state)


def backward_layer(grad_out, params, kept_state, marks, reach_back):
    attend_w, attend_b, output_w, branches, expand_w, expand_b, reduce_w, gains, offsets = params
    (
        hidden,
        normed_one,
        queries,
        window_kv,
        context,
        log_totals,
        middle,
        normed_two,
        pre_act,
        activated,
    ) = kept_state
    own_marks, window_marks = marks
    rows = hidden.shape[0]
    width = output_w.shape[0]
    bias_two = jnp.sum(grad_out, axis=0)
    grad_rounded = grad_out.astype(jnp.bfloat16)
    act_cot = contract("td,fd->tf", grad_rounded, reduce_w)
    unused, gelu_pull = jax.vjp(gelu_tanh, pre_act)
    pre_cot = gelu_pull(act_cot)[0]
    expand_bias_grad = jnp.sum(pre_cot, axis=0)
    pre_rounded = pre_cot.astype(jnp.bfloat16)
    normed_cot = tensor_total(contract("tf,df->td", pre_rounded, expand_w))
    reduce_grad = contract("tf,td->fd", activated, grad_rounded).astype(jnp.bfloat16)
    expand_grad = contract("td,tf->df", normed_two, pre_rounded).astype(jnp.bfloat16)
    unused, norm_pull = jax.vjp(layer_norm, middle, gains[1], offsets[1])
    mid_part, gain_two, offset_two = norm_pull(normed_cot)
    mid_cot = grad_out + mid_part
    bias_one = jnp.sum(mid_cot, axis=0)
    mid_rounded = mid_cot.astype(jnp.bfloat16)
    output_grad = contract("tk,td->kd", context, mid_rounded).astype(jnp.bfloat16)
    context_cot = contract("td,kd->tk", mid_rounded, output_w).astype(jnp.bfloat16)
    query_cot, kv_own, kv_back = attend_backward(
        queries, window_kv, log_totals, context_cot, own_marks, window_marks
    )
    for hop in range(1, reach_back + 1):
        begin = (reach_back - hop) * rows
        kv_own = kv_own + passed_along(kv_back[begin : begin + rows], "dp", -hop).astype(
            jnp.float32
        )
    attend_bias_grad = jnp.stack([jnp.sum(query_cot, axis=0), jnp.sum(kv_own[:, width:], axis=0)])
    proj_rounded = jnp.concatenate(
        [query_cot.astype(jnp.bfloat16), kv_own.astype(jnp.bfloat16)], axis=1
    )
    normed_cot_one = tensor_total(contract("tc,dc->td", proj_rounded, attend_w))
    attend_grad = contract("td,tc->dc", normed_one, proj_rounded).astype(jnp.bfloat16)
    unused, first_pull = jax.vjp(layer_norm, hidden, gains[0], offsets[0])
    hid_part, gain_one, offset_one = first_pull(normed_cot_one)
    in_cot = mid_cot + hid_part
    small = (
        attend_bias_grad,
        jnp.stack([bias_one, bias_two]),
        expand_bias_grad,
        jnp.stack([gain_one, gain_two]),
        jnp.stack([offset_one, offset_two]),
    )
    return (in_cot, expand_grad, reduce_grad, attend_grad, output_grad, small)


def scattered(block):
    return lax.psum_scatter(block, "dp", scatter_dimension=0, tiled=True)


def pack_output(block, model, share):
    part = model // lax.axis_size("dp")
    slabs = part // share
    owners = block.shape[0] // share
    return (
        block.reshape(owners, share, slabs, model // slabs)
        .transpose(0, 2, 1, 3)
        .reshape(owners * part, model // slabs)
    )


def unpack_output(block, model, share):
    part = model // lax.axis_size("dp")
    slabs = part // share
    owners = block.shape[0] // part
    return (
        block.reshape(owners, slabs, share, model // slabs)
        .transpose(0, 2, 1, 3)
        .reshape(owners * share, model)
    )


def split_owned(pieces, sizes, size):
    rows = [
        jnp.moveaxis(p.reshape(p.shape[:-1] + (size, p.shape[-1] // size)), -2, 0).reshape(size, -1)
        for p in pieces
    ]
    return jnp.concatenate(rows, axis=1)


def local(
    hidden_in,
    doc_ids,
    attend_weight,
    attend_bias,
    output_weight,
    branch_bias,
    expand_weight,
    expand_bias,
    reduce_weight,
    norm_gain,
    norm_bias,
    out_grad,
):
    size = lax.axis_size("dp")
    layer_count, part, three, width = attend_weight.shape
    tok_rows, model = hidden_in.shape
    share = output_weight.shape[1]
    unit_share = reduce_weight.shape[1]
    hidden_units = expand_weight.shape[2]
    reach_back = (CTX + tok_rows - 2) // tok_rows
    own_row = doc_ids + 1
    mark_list = [passed_along(own_row, "dp", hop) for hop in range(reach_back, 0, -1)]
    marks = (own_row[:, None], jnp.concatenate(mark_list + [own_row])[None, :])

    small_in = (attend_bias, branch_bias, expand_bias, norm_gain, norm_bias)
    flat = jnp.concatenate([entry.reshape(-1) for entry in small_in])
    flat_all = lax.all_gather(flat[None], "dp", axis=0, tiled=True)
    small_full = []
    at = 0
    for entry in small_in:
        piece = flat_all[:, at : at + entry.size].reshape((size,) + entry.shape)
        at += entry.size
        piece = jnp.moveaxis(piece, 0, -2)
        small_full.append(
            piece.reshape(entry.shape[:-1] + (size * entry.shape[-1],)).astype(jnp.float32)
        )
    attend_b, branches, expand_b, gains, offsets = small_full

    params = []
    for layer in range(layer_count):
        first = lax.all_gather(
            jnp.concatenate(
                [
                    attend_weight[layer].reshape(part, three * width),
                    pack_output(output_weight[layer], model, share),
                ],
                axis=1,
            ),
            "dp",
            axis=0,
            tiled=True,
        )
        second = lax.all_gather(
            jnp.concatenate(
                [expand_weight[layer], pack_output(reduce_weight[layer], model, unit_share)],
                axis=1,
            ),
            "dp",
            axis=0,
            tiled=True,
        )
        params.append(
            (
                first[:, : three * width],
                attend_b[layer],
                unpack_output(first[:, three * width :], model, share),
                branches[layer],
                second[:, :hidden_units],
                expand_b[layer],
                unpack_output(second[:, hidden_units:], model, unit_share),
                gains[layer],
                offsets[layer],
            )
        )
    saved = []
    current = hidden_in
    for layer in range(layer_count):
        current, kept_state = forward_layer(current, params[layer], marks, reach_back)
        saved.append(kept_state)
    grad_now = out_grad
    hidden_list = [None] * layer_count
    attend_list = [None] * layer_count
    small_list = [None] * layer_count
    for layer in reversed(range(layer_count)):
        grad_now, expand_grad, reduce_grad, attend_grad, output_grad, small = backward_layer(
            grad_now, params[layer], saved[layer], marks, reach_back
        )
        hidden_list[layer] = scattered(
            jnp.concatenate([expand_grad, pack_output(reduce_grad, model, unit_share)], axis=1)
        )
        small_list[layer] = small
        blocks = [attend_grad, pack_output(output_grad, model, share)]
        if layer == 0:
            stacked = [jnp.stack([entry[i] for entry in small_list]) for i in range(len(small))]
            flat_rows = split_owned(stacked, None, size).astype(jnp.bfloat16)
            count = flat_rows.shape[1]
            room = part * LANES * (-(-count // (part * LANES)))
            padded = jnp.pad(flat_rows, ((0, 0), (0, room - count)))
            blocks.append(padded.reshape(size * part, room // part))
        attend_list[layer] = scattered(jnp.concatenate(blocks, axis=1))
    hidden_out = [entry.astype(jnp.float32) for entry in hidden_list]
    attend_out = [entry.astype(jnp.float32) for entry in attend_list]
    fold = three * width
    slab = model * share // part
    tail = attend_out[0][:, fold + slab :].reshape(-1)
    small_out = []
    at = 0
    for entry in small_in:
        small_out.append(tail[at : at + entry.size].reshape(entry.shape))
        at += entry.size
    attend_bgrad, branch_bgrad, expand_bgrad, gain_grad, offset_grad = small_out
    return (
        current,
        grad_now,
        jnp.stack([entry[:, :fold].reshape(part, three, width) for entry in attend_out]),
        attend_bgrad,
        jnp.stack([unpack_output(entry[:, fold : fold + slab], model, share) for entry in attend_out]),
        branch_bgrad,
        jnp.stack([entry[:, :hidden_units] for entry in hidden_out]),
        expand_bgrad,
        jnp.stack(
            [unpack_output(entry[:, hidden_units:], model, unit_share) for entry in hidden_out]
        ),
        gain_grad,
        offset_grad,
    )


def solution(mesh):
    return jax.shard_map(
        local,
        mesh=mesh,
        in_specs=(
            P("dp", None),
            P("dp"),
            P(None, "dp", None, "tensor"),
            P(None, None, ("tensor", "dp")),
            P(None, ("tensor", "dp"), None),
            P(None, None, "dp"),
            P(None, "dp", "tensor"),
            P(None, ("tensor", "dp")),
            P(None, ("tensor", "dp"), None),
            P(None, None, "dp"),
            P(None, None, "dp"),
            P("dp", None),
        ),
        out_specs=(
            P("dp", None),
            P("dp", None),
            P(None, "dp", None, "tensor"),
            P(None, None, ("tensor", "dp")),
            P(None, ("tensor", "dp"), None),
            P(None, None, "dp"),
            P(None, "dp", "tensor"),
            P(None, ("tensor", "dp")),
            P(None, ("tensor", "dp"), None),
            P(None, None, "dp"),
            P(None, None, "dp"),
        ),
        check_vma=False,
    )
```

time: 1320 us -> 949 us (0.72)
  matrix products: 231 us -> 53.5 us
  blocking collectives: 114 us -> 10.7 us
  waiting for transfers between devices: 762 us -> 659 us
  Pallas kernels: 0 us -> 28.6 us
  other arithmetic: 75.3 us -> 57.8 us
    reduce_scatter x4 -> x0, waiting for transfers between devices: 190 us -> none  [the longest x1 52.8 us: local(): lax.psum_scatter(expand_all.astype(jnp.bfloat16), 'dp', scatter_dimension...]
    dot_general x28 -> x16, matrix products: 206 us -> 32.7 us  [contract(): jnp.einsum(pattern, left_side, right_side, preferred_element_type=jnp.flo...]
    psum x4 -> x7, waiting for transfers between devices: 175 us -> 341 us  [tensor_total(): lax.psum(partial_value.astype(jnp.bfloat16), 'tensor').astype(jnp.float32)]
    psum x3 -> x0, waiting for transfers between devices: 160 us -> none  [input_total(): lax.psum(partial_value.astype(jnp.bfloat16), 'tensor').astype(jnp.float32)]
    all_gather x12 -> x1, blocking collectives: 114 us -> 10.7 us  [local(): flat_all = lax.all_gather(flat[None], 'dp', axis=0, tiled=True)]
    ppermute x18 -> x10, waiting for transfers between devices: 0.67 us -> 39.6 us  [passed_along(): return lax.ppermute(block, axis, route)]
    unnamed x27 -> x19, waiting for transfers between devices: 132 us -> 166 us
    pallas_call x0 -> x4, Pallas kernels: none -> 28.6 us  [the longest x2 18.9 us: attend_backward(): pl.pallas_call(backward_kernel, out_shape=(jax.ShapeDtypeStruct((rows, wi...]
  transfers between devices with their start and end apart: 40 -> 25, of which waited for: 20 -> 19; matrix products, arithmetic and copies ran while one was open for 21% -> 11% of each run, Pallas kernels for 0% -> 0%
where the time goes in v1:
time: 949 us; the launch traced here: 939 us
  waiting for transfers between devices  659 us (69%)
  local copies, waits for them, and re-layouts  78.8 us (8%)
  other arithmetic  57.8 us (6%)
  matrix products  53.5 us (6%)
  starting transfers between devices  35.1 us (4%)
  Pallas kernels  28.6 us (3%)
  between operations  15.4 us (2%)
  blocking collectives  10.7 us (1%)
    psum x7, waiting for transfers between devices, tensor_total(): lax.psum(partial_value.astype(jnp.bfloat16), 'tensor').astype(jnp.float32)  341 us
    unnamed x19, waiting for transfers between devices  166 us
    all_gather x2, waiting for transfers between devices, local(): lax.all_gather(jnp.concatenate([expand_weight[layer], pack_output(reduce_...  68.9 us
    unnamed x186, local copies, waits for them, and re-layouts  56.3 us
    all_gather x2, waiting for transfers between devices, local(): lax.all_gather(jnp.concatenate([attend_weight[layer].reshape(part, three...  44 us
    ppermute x10, waiting for transfers between devices, passed_along(): return lax.ppermute(block, axis, route)  39.6 us
    dot_general x16, matrix products, contract(): jnp.einsum(pattern, left_side, right_side, preferred_element_type=jnp.flo...  32.7 us
    ppermute x10, starting transfers between devices, passed_along(): return lax.ppermute(block, axis, route)  22.7 us
  transfers between devices with their start and end apart: 25, of which 19 were waited for; matrix products, arithmetic and copies ran while one was open for 11% of the time, Pallas kernels for 0%

profile of v1, /device:TPU:0, one launch (start us, length us, event | category | flops | bytes accessed | tf_op | source)
XLA Modules:
  0.0 938.8 jit_solution(13363254178949113065)
XLA Ops:
  11.7 10.7 %all-gather.1 = bf16[8,1,1920]{2,1,0:T(2,128)(2,1)S(1)} all-gather(bf16[1,1,1920]{2,1,0:T(2,128)(2,1)S(1)} %reshape.419), channel_id=2, replica_groups=mesh['dp'=8,'tensor'=4] {'dp'}, dimensions={0}, use_global_device_ids=true | all-gather | bytes 34560 | tf_op jit(solution)/shard_map/all_gather | solution.py:338
  23.3 18.1 %all-gather.7.cloned.1.call-done = bf16[1024,1024]{0,1:T(8,128)(2,1)} async-done(((bf16[128,1024]{0,1:T(8,128)(2,1)}), bf16[1024,1024]{0,1:T(8,128)(2,1)}) %all-gather.7.cloned.1.call-update) | async-done | bytes 2097168 | tf_op jit(solution)/shard_map/all_gather | solution.py:352
  46.4 4.1 collective-permute-start
  55.4 6.7 collective-permute-done.2
  65.4 4.9 attend_forward.2
  75.3 11.2 %all-reduce.14.cloned.1.call-start = ((), (), s32[]{:S(2)}) async-start(), calls=%async_computation.7 | async-start | bytes 2097152 | tf_op jit(solution)/shard_map/psum | solution.py:179
  87.1 41.9 %all-reduce.12.cloned.1.call-done = bf16[512,1024]{1,0:T(8,128)(2,1)} async-done(((bf16[512,1024]{1,0:T(8,128)(2,1)}), bf16[512,1024]{1,0:T(8,128)(2,1)}) %all-reduce.12.cloned.1.call-update) | async-done | bytes 1048592 | tf_op jit(solution)/shard_map/psum | solution.py:179
  132.9 34.5 %all-gather.9.cloned.1.call-done = bf16[1024,2048]{1,0:T(8,128)(2,1)} async-done(((bf16[128,2048]{1,0:T(8,128)(2,1)}), bf16[1024,2048]{1,0:T(8,128)(2,1)}) %all-gather.9.cloned.1.call-update) | async-done | bytes 4194320 | tf_op jit(solution)/shard_map/all_gather | solution.py:364
  167.3 3.7 fusion.43
  176.1 50.9 %all-reduce.14.cloned.1.call-done = bf16[512,1024]{1,0:T(8,128)(2,1)} async-done(((bf16[512,1024]{1,0:T(8,128)(2,1)}), bf16[512,1024]{1,0:T(8,128)(2,1)}) %all-reduce.14.cloned.1.call-update) | async-done | bytes 1048592 | tf_op jit(solution)/shard_map/psum | solution.py:179
  230.8 25.8 %all-gather.11.cloned.1.call-done = bf16[1024,1024]{0,1:T(8,128)(2,1)} async-done(((bf16[128,1024]{0,1:T(8,128)(2,1)}), bf16[1024,1024]{0,1:T(8,128)(2,1)}) %all-gather.11.cloned.1.call-update) | async-done | bytes 2097168 | tf_op jit(solution)/shard_map/all_gather | solution.py:352
  268.4 9.4 %collective-permute-done.4 = bf16[512,512]{1,0:T(8,128)(2,1)} collective-permute-done((bf16[512,512]{1,0:T(8,128)(2,1)S(1)}, bf16[512,512]{1,0:T(8,128)(2,1)}, u32[]{:S(2)}, u32[]{:S(2)}) %collective-permute-start.4) | collective-permute-done | bytes 524320 | tf_op jit(solution)/shard_map/ppermute | solution.py:20
  279.3 4.9 attend_forward.3
  289.0 54.1 %all-reduce.16.cloned.1.call-done = bf16[512,1024]{1,0:T(8,128)(2,1)} async-done(((bf16[512,1024]{1,0:T(8,128)(2,1)}), bf16[512,1024]{1,0:T(8,128)(2,1)}) %all-reduce.16.cloned.1.call-update) | async-done | bytes 1048592 | tf_op jit(solution)/shard_map/psum | solution.py:179
  347.0 34.5 %all-gather.13.cloned.1.call-done = bf16[1024,2048]{1,0:T(8,128)(2,1)} async-done(((bf16[128,2048]{1,0:T(8,128)(2,1)}), bf16[1024,2048]{1,0:T(8,128)(2,1)}) %all-gather.13.cloned.1.call-update) | async-done | bytes 4194320 | tf_op jit(solution)/shard_map/all_gather | solution.py:364
  381.5 3.7 fusion.35
  392.3 51.6 %all-reduce.18.cloned.1.call-done = bf16[512,1024]{1,0:T(8,128)(2,1)} async-done(((bf16[512,1024]{1,0:T(8,128)(2,1)}), bf16[512,1024]{1,0:T(8,128)(2,1)}) %all-reduce.18.cloned.1.call-update) | async-done | bytes 1048592 | tf_op jit(solution)/shard_map/psum | solution.py:179
  450.4 9.3 attend_backward.2
  462.5 12.9 %collective-permute-done.7 = bf16[512,512]{1,0:T(8,128)(2,1)S(1)} collective-permute-done((bf16[512,512]{1,0:T(8,128)(2,1)S(1)}, bf16[512,512]{1,0:T(8,128)(2,1)S(1)}, u32[]{:S(2)}, u32[]{:S(2)}) %collective-permute-start.7) | collective-permute-done | bytes 524320 | tf_op jit(solution)/shard_map/ppermute | solution.py:20
  479.5 56.3 %all-reduce.20.cloned.1.call-done = bf16[512,1024]{1,0:T(8,128)(2,1)} async-done(((bf16[512,1024]{1,0:T(8,128)(2,1)}), bf16[512,1024]{1,0:T(8,128)(2,1)}) %all-reduce.20.cloned.1.call-update) | async-done | bytes 1048592 | tf_op jit(solution)/shard_map/psum | solution.py:179
  549.1 51.3 %all-reduce.22.cloned.1.call-done = bf16[512,1024]{1,0:T(8,128)(2,1)} async-done(((bf16[512,1024]{1,0:T(8,128)(2,1)}), bf16[512,1024]{1,0:T(8,128)(2,1)}) %all-reduce.22.cloned.1.call-update) | async-done | bytes 1048592 | tf_op jit(solution)/shard_map/psum | solution.py:179
  606.8 9.5 %attend_backward.3 = (f32[512,256]{1,0:T(8,128)S(1)}, f32[512,512]{1,0:T(8,128)S(1)}, bf16[1024,512]{1,0:T(8,128)(2,1)S(1)}) custom-call(bf16[512,256]{1,0:T(8,128)(2,1)S(1)} %copy-done.1, bf16[1536,512]{1,0:T(8,128)(2,1)S(1)} %pad_maximum_fusion.4.kv_ref, f32[512,4]{1,0:T(8,128)S(1)} %copy-done.9, bf16[512,256]{1,0:T(8,128)(2,1)S(1)} %convolution_convert_fusion.12.cot_ref, ...), custom_call_target="tpu_custom_call" | custom-call | tf_op jit(solution)/shard_map/attend_backward/pallas_call | solution.py:163
  621.7 10.4 %collective-permute-done.9 = bf16[512,512]{1,0:T(8,128)(2,1)S(1)} collective-permute-done((bf16[512,512]{1,0:T(8,128)(2,1)S(1)}, bf16[512,512]{1,0:T(8,128)(2,1)S(1)}, u32[]{:S(2)}, u32[]{:S(2)}) %collective-permute-start.9) | collective-permute-done | bytes 524320 | tf_op jit(solution)/shard_map/ppermute | solution.py:20
  651.9 6.5 copy.161
  666.8 6.5 copy.159
  688.2 4.1 convolution_convert_fusion.5
  692.3 34.5 %all-reduce.24.cloned.1.call-done = (bf16[512,1024]{1,0:T(8,128)(2,1)}, bf16[512,1024]{1,0:T(8,128)(2,1)}) async-done(((bf16[512,1024]{1,0:T(8,128)(2,1)}, bf16[512,1024]{1,0:T(8,128)(2,1)}), (bf16[512,1024]{1,0:T(8,128)(2,1)}, bf16[512,1024]{1,0:T(8,128)(2,1)})) %all-reduce.24.cloned.1.call-update) | async-done | bytes 2097168 | tf_op jit(solution)/shard_map/psum | solution.py:179
  737.8 4.4 copy.155
  742.2 28.4 %reduce-scatter.15.cloned.1.call-done = bf16[128,1024]{1,0:T(8,128)(2,1)} async-done(((bf16[1024,1024]{1,0:T(8,128)(2,1)}), bf16[128,1024]{1,0:T(8,128)(2,1)}) %reduce-scatter.15.cloned.1.call-update) | async-done | bytes 262160
  773.6 51.6 %reduce-scatter.19.cloned.1.call-done = bf16[128,2048]{1,0:T(8,128)(2,1)} async-done(((bf16[1024,2048]{1,0:T(8,128)(2,1)}), bf16[128,2048]{1,0:T(8,128)(2,1)}) %reduce-scatter.19.cloned.1.call-update) | async-done | bytes 524304
  834.5 45.1 %reduce-scatter.17.cloned.1.call-done = bf16[128,2048]{1,0:T(8,128)(2,1)} async-done(((bf16[1024,2048]{1,0:T(8,128)(2,1)}), bf16[128,2048]{1,0:T(8,128)(2,1)}) %reduce-scatter.17.cloned.1.call-update) | async-done | bytes 524304
  884.8 40.4 %reduce-scatter.13.cloned.1.call-done = bf16[128,1152]{1,0:T(8,128)(2,1)} async-done(((bf16[1024,1152]{1,0:T(8,128)(2,1)}), bf16[128,1152]{1,0:T(8,128)(2,1)}) %reduce-scatter.13.cloned.1.call-update) | async-done | bytes 294928
  (399 shorter events, 181.3 us)
Async XLA Ops:
  7.2 15.5 %copy-start.20 = (f32[512,1024]{1,0:T(8,128)S(1)}, f32[512,1024]{1,0:T(8,128)}, u32[]{:S(2)}) copy-start(f32[512,1024]{1,0:T(8,128)} %param.12) | copy-start | bytes 6291460
  7.2 34.2 %all-gather.7.cloned.1.call-start = ((), (), s32[]{:S(2)}) async-start(), calls=%async_computation.4 | async-start | bytes 2359296 | tf_op jit(solution)/shard_map/all_gather | solution.py:352
  10.5 118.5 %all-reduce.12.cloned.1.call-start = ((), (), s32[]{:S(2)}) async-start(), calls=%async_computation.5 | async-start | bytes 2097152 | tf_op jit(solution)/shard_map/psum | solution.py:179
  44.0 18.1 %slice-start = ((bf16[1024,1024]{0,1:T(8,128)(2,1)}), bf16[1024,256]{0,1:T(8,128)(2,1)S(1)}, s32[]{:S(2)}) async-start(bf16[1024,1024]{0,1:T(8,128)(2,1)} %all-gather.7.cloned.1.call-done), calls=%async_computation.19 | async-start | bytes 1048576 | tf_op jit(solution)/shard_map/slice | solution.py:377
  44.1 20.1 %collective-permute-start.1 = (bf16[512,512]{1,0:T(8,128)(2,1)S(1)}, bf16[512,512]{1,0:T(8,128)(2,1)S(1)}, u32[]{:S(2)}, u32[]{:S(2)}) collective-permute-start(bf16[512,512]{1,0:T(8,128)(2,1)S(1)} %fusion.68), channel_id=1, source_target_pairs={{0,4},{4,8},{8,12},{12,16},{16,20},{20,24},{24,28},{1,5},{5,9},{9,... | collective-permute-start | bytes 1572872 | tf_op jit(solution)/shard_map/ppermute | solution.py:20
  46.4 17.8 %collective-permute-start = (bf16[512,512]{1,0:T(8,128)(2,1)S(1)}, bf16[512,512]{1,0:T(8,128)(2,1)}, u32[]{:S(2)}, u32[]{:S(2)}) collective-permute-start(bf16[512,512]{1,0:T(8,128)(2,1)S(1)} %fusion.68), channel_id=1, source_target_pairs={{0,8},{4,12},{8,16},{12,20},{16,24},{20,28},{1,9},{5,13},{9,17},{1... | collective-permute-start | bytes 1572872 | tf_op jit(solution)/shard_map/ppermute | solution.py:20
  50.6 4.8 collective-permute-start.3
  53.2 8.9 collective-permute-start.2
  72.4 94.9 %all-gather.9.cloned.1.call-start = ((), (), s32[]{:S(2)}) async-start(), calls=%async_computation.6 | async-start | bytes 4718592 | tf_op jit(solution)/shard_map/all_gather | solution.py:364
  75.3 151.6 %all-reduce.14.cloned.1.call-start = ((), (), s32[]{:S(2)}) async-start(), calls=%async_computation.7 | async-start | bytes 2097152 | tf_op jit(solution)/shard_map/psum | solution.py:179
  174.9 81.8 %all-gather.11.cloned.1.call-start = ((), (), s32[]{:S(2)}) async-start(), calls=%async_computation.8 | async-start | bytes 2359296 | tf_op jit(solution)/shard_map/all_gather | solution.py:352
  176.0 167.1 %all-reduce.16.cloned.1.call-start = ((), (), s32[]{:S(2)}) async-start(), calls=%async_computation.9 | async-start | bytes 2097152 | tf_op jit(solution)/shard_map/psum | solution.py:179
  259.9 8.5 collective-permute-start.5
  263.0 14.8 %collective-permute-start.4 = (bf16[512,512]{1,0:T(8,128)(2,1)S(1)}, bf16[512,512]{1,0:T(8,128)(2,1)}, u32[]{:S(2)}, u32[]{:S(2)}) collective-permute-start(bf16[512,512]{1,0:T(8,128)(2,1)S(1)} %fusion.67), channel_id=1, source_target_pairs={{0,8},{4,12},{8,16},{12,20},{16,24},{20,28},{1,9},{5,13},{9,17},{1... | collective-permute-start | bytes 1572872 | tf_op jit(solution)/shard_map/ppermute | solution.py:20
  267.1 17.8 %copy-start.39 = (bf16[32,8,4,256]{3,1,2,0:T(8,128)(2,1)}, bf16[32,8,4,256]{3,1,2,0:T(8,128)(2,1)S(1)}, u32[]{:S(2)}) copy-start(bf16[32,8,4,256]{3,1,2,0:T(8,128)(2,1)S(1)} %copy.169) | copy-start | bytes 1572868
  268.4 15.8 %copy-start.2 = (bf16[512,256]{1,0:T(8,128)(2,1)}, bf16[512,256]{1,0:T(8,128)(2,1)S(1)}, u32[]{:S(2)}) copy-start(bf16[512,256]{1,0:T(8,128)(2,1)S(1)} %fusion.69.q_ref) | copy-start | bytes 786436
  287.1 94.4 %all-gather.13.cloned.1.call-start = ((), (), s32[]{:S(2)}) async-start(), calls=%async_computation.10 | async-start | bytes 4718592 | tf_op jit(solution)/shard_map/all_gather | solution.py:364
  289.0 154.9 %all-reduce.18.cloned.1.call-start = ((), (), s32[]{:S(2)}) async-start(), calls=%async_computation.11 | async-start | bytes 2097152 | tf_op jit(solution)/shard_map/psum | solution.py:179
  391.9 144.0 %all-reduce.20.cloned.1.call-start = ((), (), s32[]{:S(2)}) async-start(), calls=%async_computation.12 | async-start | bytes 2097152 | tf_op jit(solution)/shard_map/psum | solution.py:179
  459.8 15.7 %collective-permute-start.7 = (bf16[512,512]{1,0:T(8,128)(2,1)S(1)}, bf16[512,512]{1,0:T(8,128)(2,1)S(1)}, u32[]{:S(2)}, u32[]{:S(2)}) collective-permute-start(bf16[512,512]{1,0:T(8,128)(2,1)S(1)} %get-tuple-element.120), channel_id=1, source_target_pairs={{8,0},{12,4},{16,8},{20,12},{24,16},{28,20},{9,1},{13,5},{17,9},{2... | collective-permute-start | bytes 1572872 | tf_op jit(solution)/shard_map/ppermute | solution.py:20
  461.1 14.4 %collective-permute-start.6 = (bf16[512,512]{1,0:T(8,128)(2,1)S(1)}, bf16[512,512]{1,0:T(8,128)(2,1)S(1)}, u32[]{:S(2)}, u32[]{:S(2)}) collective-permute-start(bf16[512,512]{1,0:T(8,128)(2,1)S(1)} %get-tuple-element.119), channel_id=1, source_target_pairs={{4,0},{8,4},{12,8},{16,12},{20,16},{24,20},{28,24},{5,1},{9,5},{13... | collective-permute-start | bytes 1572872 | tf_op jit(solution)/shard_map/ppermute | solution.py:20
  462.4 15.1 %copy-start.45 = (bf16[1024,1024]{0,1:T(8,128)(2,1)S(1)}, bf16[1024,1024]{0,1:T(8,128)(2,1)}, u32[]{:S(2)}) copy-start(bf16[1024,1024]{0,1:T(8,128)(2,1)} %all-gather.11.cloned.1.call-done) | copy-start | bytes 6291460
  479.5 120.9 %all-reduce.22.cloned.1.call-start = ((), (), s32[]{:S(2)}) async-start(), calls=%async_computation.13 | async-start | bytes 2097152 | tf_op jit(solution)/shard_map/psum | solution.py:179
  549.1 177.7 %all-reduce.24.cloned.1.call-start = ((), (), s32[]{:S(2)}) async-start(), calls=%async_computation.18 | async-start | bytes 4194304 | tf_op jit(solution)/shard_map/psum | solution.py:179
  616.4 15.7 %collective-permute-start.9 = (bf16[512,512]{1,0:T(8,128)(2,1)S(1)}, bf16[512,512]{1,0:T(8,128)(2,1)S(1)}, u32[]{:S(2)}, u32[]{:S(2)}) collective-permute-start(bf16[512,512]{1,0:T(8,128)(2,1)S(1)} %get-tuple-element.118), channel_id=1, source_target_pairs={{8,0},{12,4},{16,8},{20,12},{24,16},{28,20},{9,1},{13,5},{17,9},{2... | collective-permute-start | bytes 1572872 | tf_op jit(solution)/shard_map/ppermute | solution.py:20
  617.7 14.4 %collective-permute-start.8 = (bf16[512,512]{1,0:T(8,128)(2,1)S(1)}, bf16[512,512]{1,0:T(8,128)(2,1)S(1)}, u32[]{:S(2)}, u32[]{:S(2)}) collective-permute-start(bf16[512,512]{1,0:T(8,128)(2,1)S(1)} %get-tuple-element.117), channel_id=1, source_target_pairs={{4,0},{8,4},{12,8},{16,12},{20,16},{24,20},{28,24},{5,1},{9,5},{13... | collective-permute-start | bytes 1572872 | tf_op jit(solution)/shard_map/ppermute | solution.py:20
  636.1 134.5 %reduce-scatter.15.cloned.1.call-start = ((), (), s32[]{:S(2)}) async-start(), calls=%async_computation.15 | async-start | bytes 2359296
  644.1 181.1 %reduce-scatter.19.cloned.1.call-start = ((), (), s32[]{:S(2)}) async-start(), calls=%async_computation.17 | async-start | bytes 4718592
  658.4 221.2 %reduce-scatter.17.cloned.1.call-start = ((), (), s32[]{:S(2)}) async-start(), calls=%async_computation.16 | async-start | bytes 4718592
  673.3 251.9 %reduce-scatter.13.cloned.1.call-start = ((), (), s32[]{:S(2)}) async-start(), calls=%async_computation.14 | async-start | bytes 2654208
  772.5 55.9 %copy-start.59 = (f32[512]{0:T(512)S(1)}, f32[512]{0:T(512)}, u32[]{:S(2)}) copy-start(f32[512]{0:T(512)} %get-tuple-element.87) | copy-start | bytes 6148
  883.5 43.2 %copy-start.51 = (f32[128,768]{0,1:T(8,128)S(1)}, f32[128,768]{0,1:T(8,128)}, u32[]{:S(2)}) copy-start(f32[128,768]{0,1:T(8,128)} %copy.174) | copy-start | bytes 1179652
  (75 other events, 282.3 us)
Sparse Core Ops, SparseCore 0:
  10.6 30.8 all-gather.6
  72.6 56.3 all-reduce.11
  131.5 35.8 all-gather.8
  175.0 51.8 all-reduce.13
  229.2 27.3 all-gather.10
  287.2 55.9 all-reduce.15
  345.6 35.8 all-gather.12
  392.0 51.8 all-reduce.17
  479.6 56.2 all-reduce.19
  549.2 51.1 all-reduce.21
  636.2 90.4 all-reduce.23
  730.5 40.1 reduce-scatter.14
  774.0 51.1 reduce-scatter.18
  828.4 51.1 reduce-scatter.16
  882.8 42.3 reduce-scatter.12

commit v2 on v1

--- a/solution.py
+++ b/solution.py
@@ -175,8 +175,102 @@
     )(queries, window_kv, log_totals, out_cot, own_marks, window_marks)
 
 
+def line_kernel(chunks, x_ref, o_ref, from_near, from_mid, pair, total, near_send, mid_send, near_recv, mid_recv):
+    place = lax.axis_index("tensor")
+    near = place + 1 - 2 * lax.rem(place, 2)
+    across = 3 - place
+    is_end = (place == 0) | (place == 3)
+    is_mid = (place == 1) | (place == 2)
+    step = x_ref.shape[0] // chunks
+    barrier = pltpu.get_barrier_semaphore()
+
+    def part(ref, c):
+        return ref.at[pl.ds(c * step, step)]
+
+    def to_near(src, c):
+        return pltpu.make_async_remote_copy(
+            src_ref=part(src, c),
+            dst_ref=part(from_near, c),
+            send_sem=near_send.at[c],
+            recv_sem=near_recv.at[c],
+            device_id={"tensor": near},
+            device_id_type=pl.DeviceIdType.MESH,
+        )
+
+    def to_mid(c):
+        return pltpu.make_async_remote_copy(
+            src_ref=part(pair, c),
+            dst_ref=part(from_mid, c),
+            send_sem=mid_send.at[c],
+            recv_sem=mid_recv.at[c],
+            device_id={"tensor": across},
+            device_id_type=pl.DeviceIdType.MESH,
+        )
+
+    def added(left, right, c):
+        rows = pl.ds(c * step, step)
+        both = left[rows, :].astype(jnp.float32) + right[rows, :].astype(jnp.float32)
+        return both.astype(jnp.bfloat16)
+
+    pl.semaphore_signal(
+        barrier, inc=1, device_id={"tensor": near}, device_id_type=pl.DeviceIdType.MESH
+    )
+
+    @pl.when(is_end)
+    def _():
+        pl.semaphore_wait(barrier, 1)
+        for c in range(chunks):
+            to_near(x_ref, c).start()
+        for c in range(chunks):
+            to_near(x_ref, c).wait_recv()
+            rows = pl.ds(c * step, step)
+            o_ref[rows, :] = from_near[rows, :]
+        for c in range(chunks):
+            to_near(x_ref, c).wait_send()
+
+    @pl.when(is_mid)
+    def _():
+        pl.semaphore_signal(
+            barrier, inc=1, device_id={"tensor": across}, device_id_type=pl.DeviceIdType.MESH
+        )
+        pl.semaphore_wait(barrier, 2)
+        lag = 2
+        for c in range(chunks + lag):
+            if c < chunks:
+                to_near(total, c).wait_recv()
+                pair[pl.ds(c * step, step), :] = added(x_ref, from_near, c)
+                to_mid(c).start()
+            done = c - lag
+            if done >= 0:
+                to_mid(done).wait_recv()
+                result = added(pair, from_mid, done)
+                total[pl.ds(done * step, step), :] = result
+                to_near(total, done).start()
+                o_ref[pl.ds(done * step, step), :] = result
+        for c in range(chunks):
+            to_mid(c).wait_send()
+            to_near(total, c).wait_send()
+
+
 def tensor_total(partial_value):
-    return lax.psum(partial_value.astype(jnp.bfloat16), "tensor").astype(jnp.float32)
+    rounded = partial_value.astype(jnp.bfloat16)
+    rows = rounded.shape[0]
+    if lax.axis_size("tensor") != 4 or rows % 128:
+        return lax.psum(rounded, "tensor").astype(jnp.float32)
+    chunks = 8
+    block = pltpu.VMEM(rounded.shape, jnp.bfloat16)
+    summed = pl.pallas_call(
+        functools.partial(line_kernel, chunks),
+        out_shape=jax.ShapeDtypeStruct(rounded.shape, jnp.bfloat16),
+        in_specs=in_vmem(1),
+        out_specs=in_vmem(1)[0],
+        scratch_shapes=[block] * 4 + [pltpu.SemaphoreType.DMA((chunks,))] * 4,
+        compiler_params=pltpu.CompilerParams(
+            collective_id=0, has_side_effects=True, vmem_limit_bytes=24 * 1024 * 1024
+        ),
+        name="line_total",
+    )(rounded)
+    return summed.astype(jnp.float32)
 
 
 def forward_layer(hidden, params, marks, reach_back):
@@ -247,6 +341,9 @@
     mid_rounded = mid_cot.astype(jnp.bfloat16)
     output_grad = contract("tk,td->kd", context, mid_rounded).astype(jnp.bfloat16)
     context_cot = contract("td,kd->tk", mid_rounded, output_w).astype(jnp.bfloat16)
+    context_cot, expand_grad, reduce_grad = lax.optimization_barrier(
+        (context_cot, expand_grad, reduce_grad)
+    )
     query_cot, kv_own, kv_back = attend_backward(
         queries, window_kv, log_totals, context_cot, own_marks, window_marks
     )
@@ -408,7 +505,10 @@
             room = part * LANES * (-(-count // (part * LANES)))
             padded = jnp.pad(flat_rows, ((0, 0), (0, room - count)))
             blocks.append(padded.reshape(size * part, room // part))
-        attend_list[layer] = scattered(jnp.concatenate(blocks, axis=1))
+        packed = jnp.concatenate(blocks, axis=1)
+        if layer > 0:
+            grad_now, packed = lax.optimization_barrier((grad_now, packed))
+        attend_list[layer] = scattered(packed)
     hidden_out = [entry.astype(jnp.float32) for entry in hidden_list]
     attend_out = [entry.astype(jnp.float32) for entry in attend_list]
     fold = three * width

time: 949 us -> 709 us (0.75)
  waiting for transfers between devices: 659 us -> 189 us
  Pallas kernels: 28.6 us -> 302 us
  local copies, waits for them, and re-layouts: 78.8 us -> 43.1 us
    psum x7 -> x0, waiting for transfers between devices: 341 us -> none  [tensor_total(): lax.psum(partial_value.astype(jnp.bfloat16), 'tensor').astype(jnp.float32)]
    pallas_call x0 -> x8, Pallas kernels: none -> 274 us  [tensor_total(): pl.pallas_call(functools.partial(line_kernel, chunks), out_shape=jax.Shap...]
    unnamed x19 -> x10, waiting for transfers between devices: 166 us -> 35.6 us
    reduce_scatter x0 -> x2, waiting for transfers between devices: none -> 101 us  [scattered(): return lax.psum_scatter(block, 'dp', scatter_dimension=0, tiled=True)]
    all_gather x2, waiting for transfers between devices: 68.9 us -> 0.04 us  [local(): lax.all_gather(jnp.concatenate([expand_weight[layer], pack_output(reduce_...]
    all_gather x2, waiting for transfers between devices: 44 us -> 9.6 us  [local(): lax.all_gather(jnp.concatenate([attend_weight[layer].reshape(part, three...]
    unnamed x186 -> x126, local copies, waits for them, and re-layouts: 56.3 us -> 22.2 us
    psum x7 -> x0, starting transfers between devices: 11.8 us -> none  [tensor_total(): lax.psum(partial_value.astype(jnp.bfloat16), 'tensor').astype(jnp.float32)]
  transfers between devices with their start and end apart: 25 -> 18, of which waited for: 19 -> 8; matrix products, arithmetic and copies ran while one was open for 11% -> 12% of each run, Pallas kernels for 0% -> 21%
where the time goes in v2:
time: 709 us; the launch traced here: 699 us
  Pallas kernels  302 us (43%)
  waiting for transfers between devices  189 us (27%)
  other arithmetic  64.1 us (9%)
  matrix products  49.1 us (7%)
  local copies, waits for them, and re-layouts  43.1 us (6%)
  starting transfers between devices  26.4 us (4%)
  between operations  15.8 us (2%)
  blocking collectives  9.27 us (1%)
    pallas_call x8, Pallas kernels, tensor_total(): pl.pallas_call(functools.partial(line_kernel, chunks), out_shape=jax.Shap...  274 us
    reduce_scatter x2, waiting for transfers between devices, scattered(): return lax.psum_scatter(block, 'dp', scatter_dimension=0, tiled=True)  101 us
    ppermute x10, waiting for transfers between devices, passed_along(): return lax.ppermute(block, axis, route)  42.9 us
    unnamed x10, waiting for transfers between devices  35.6 us
    dot_general x16, matrix products, contract(): jnp.einsum(pattern, left_side, right_side, preferred_element_type=jnp.flo...  32.6 us
    ppermute x10, starting transfers between devices, passed_along(): return lax.ppermute(block, axis, route)  26 us
    unnamed x126, local copies, waits for them, and re-layouts  22.2 us
    pallas_call x2, Pallas kernels, attend_backward(): pl.pallas_call(backward_kernel, out_shape=(jax.ShapeDtypeStruct((rows, wi...  18.5 us
  transfers between devices with their start and end apart: 18, of which 8 were waited for; matrix products, arithmetic and copies ran while one was open for 12% of the time, Pallas kernels for 21%

profile of v2, /device:TPU:0, one launch (start us, length us, event | category | flops | bytes accessed | tf_op | source)
XLA Modules:
  0.0 698.9 jit_solution(12524603855165419283)
XLA Ops:
  15.1 4.4 collective-permute-start.2
  21.5 9.3 %all-gather.1 = bf16[8,1,1920]{2,1,0:T(2,128)(2,1)S(1)} all-gather(bf16[1,1,1920]{2,1,0:T(2,128)(2,1)S(1)} %reshape.419), channel_id=2, replica_groups=mesh['dp'=8,'tensor'=4] {'dp'}, dimensions={0}, use_global_device_ids=true | all-gather | bytes 34560 | tf_op jit(solution)/shard_map/all_gather | solution.py:435
  31.8 9.6 %all-gather.7.cloned.1.call-done = bf16[1024,1024]{0,1:T(8,128)(2,1)} async-done(((bf16[128,1024]{0,1:T(8,128)(2,1)}), bf16[1024,1024]{0,1:T(8,128)(2,1)}) %all-gather.7.cloned.1.call-update) | async-done | bytes 2097168 | tf_op jit(solution)/shard_map/all_gather | solution.py:449
  46.3 3.4 collective-permute-start
  52.0 15.6 %collective-permute-done = bf16[512,512]{1,0:T(8,128)(2,1)S(1)} collective-permute-done((bf16[512,512]{1,0:T(8,128)(2,1)S(1)}, bf16[512,512]{1,0:T(8,128)(2,1)S(1)}, u32[]{:S(2)}, u32[]{:S(2)}) %collective-permute-start) | collective-permute-done | bytes 524320 | tf_op jit(solution)/shard_map/ppermute | solution.py:20
  67.7 4.9 attend_forward.2
  73.0 36.4 %line_total.8 = bf16[512,1024]{1,0:T(8,128)(2,1)S(1)} custom-call(bf16[512,1024]{1,0:T(8,128)(2,1)S(1)} %convolution_convert_fusion.9.x_ref), custom_call_target="tpu_custom_call" | custom-call | tf_op jit(solution)/shard_map/line_total/pallas_call | solution.py:262
  116.4 35.5 %line_total.9 = bf16[512,1024]{1,0:T(8,128)(2,1)S(1)} custom-call(bf16[512,1024]{1,0:T(8,128)(2,1)S(1)} %fusion.48.x_ref), custom_call_target="tpu_custom_call" | custom-call | tf_op jit(solution)/shard_map/line_total/pallas_call | solution.py:262
  160.9 5.9 collective-permute-start.4
  169.7 8.6 %collective-permute-done.4 = bf16[512,512]{1,0:T(8,128)(2,1)} collective-permute-done((bf16[512,512]{1,0:T(8,128)(2,1)S(1)}, bf16[512,512]{1,0:T(8,128)(2,1)}, u32[]{:S(2)}, u32[]{:S(2)}) %collective-permute-start.4) | collective-permute-done | bytes 524320 | tf_op jit(solution)/shard_map/ppermute | solution.py:20
  179.8 4.9 attend_forward.3
  185.2 34.5 %line_total.10 = bf16[512,1024]{1,0:T(8,128)(2,1)S(1)} custom-call(bf16[512,1024]{1,0:T(8,128)(2,1)S(1)} %convolution_convert_fusion.8.x_ref), custom_call_target="tpu_custom_call" | custom-call | tf_op jit(solution)/shard_map/line_total/pallas_call | solution.py:262
  224.8 3.7 fusion.35
  234.6 4.4 convolution_convert_fusion.3
  240.3 35.8 %line_total.12 = bf16[512,1024]{1,0:T(8,128)(2,1)S(1)} custom-call(bf16[512,1024]{1,0:T(8,128)(2,1)S(1)} %fusion.51.x_ref), custom_call_target="tpu_custom_call" | custom-call | tf_op jit(solution)/shard_map/line_total/pallas_call | solution.py:262
  282.5 35.2 %line_total.11 = bf16[512,1024]{1,0:T(8,128)(2,1)S(1)} custom-call(bf16[512,1024]{1,0:T(8,128)(2,1)S(1)} %fusion.54.x_ref), custom_call_target="tpu_custom_call" | custom-call | tf_op jit(solution)/shard_map/line_total/pallas_call | solution.py:262
  317.7 3.5 fusion.96
  322.3 9.2 %attend_backward.2 = (f32[512,256]{1,0:T(8,128)S(1)}, f32[512,512]{1,0:T(8,128)S(1)}, bf16[1024,512]{1,0:T(8,128)(2,1)S(1)}) custom-call(bf16[512,256]{1,0:T(8,128)(2,1)S(1)} %fusion.69.q_ref, bf16[1536,512]{1,0:T(8,128)(2,1)S(1)} %pad_maximum_fusion.5.kv_ref, f32[512,4]{1,0:T(8,128)S(1)} %copy-done.15, ...), custom_call_target="tpu_custom_call" | custom-call | tf_op jit(solution)/shard_map/attend_backward/pallas_call | solution.py:163
  342.8 7.6 %collective-permute-done.7 = bf16[512,512]{1,0:T(8,128)(2,1)} collective-permute-done((bf16[512,512]{1,0:T(8,128)(2,1)}, bf16[512,512]{1,0:T(8,128)(2,1)}, u32[]{:S(2)}, u32[]{:S(2)}) %collective-permute-start.7) | collective-permute-done | bytes 524320 | tf_op jit(solution)/shard_map/ppermute | solution.py:20
  356.7 31.7 %line_total.13 = bf16[512,1024]{1,0:T(8,128)(2,1)S(1)} custom-call(bf16[512,1024]{1,0:T(8,128)(2,1)S(1)} %convolution_convert_fusion.7.x_ref), custom_call_target="tpu_custom_call" | custom-call | tf_op jit(solution)/shard_map/line_total/pallas_call | solution.py:262
  408.1 33.2 %line_total.14 = bf16[512,1024]{1,0:T(8,128)(2,1)S(1)} custom-call(bf16[512,1024]{1,0:T(8,128)(2,1)S(1)} %fusion.45.x_ref), custom_call_target="tpu_custom_call" | custom-call | tf_op jit(solution)/shard_map/line_total/pallas_call | solution.py:262
  446.1 9.4 %attend_backward.3 = (f32[512,256]{1,0:T(8,128)S(1)}, f32[512,512]{1,0:T(8,128)S(1)}, bf16[1024,512]{1,0:T(8,128)(2,1)S(1)}) custom-call(bf16[512,256]{1,0:T(8,128)(2,1)S(1)} %fusion.70.q_ref, bf16[1536,512]{1,0:T(8,128)(2,1)S(1)} %copy-done.1, f32[512,4]{1,0:T(8,128)S(1)} %copy-done.13, bf16[512,256]{1,0:T(8,128)(2,1)S(1)} %convolution_convert_fusion.12.cot_ref, ...), custom_call_target="tpu_custom_call" | custom-call | tf_op jit(solution)/shard_map/attend_backward/pallas_call | solution.py:163
  460.8 3.9 copy.147
  470.1 11.1 %collective-permute-done.9 = bf16[512,512]{1,0:T(8,128)(2,1)} collective-permute-done((bf16[512,512]{1,0:T(8,128)(2,1)}, bf16[512,512]{1,0:T(8,128)(2,1)}, u32[]{:S(2)}, u32[]{:S(2)}) %collective-permute-start.9) | collective-permute-done | bytes 524320 | tf_op jit(solution)/shard_map/ppermute | solution.py:20
  484.5 31.5 %line_total.15 = bf16[512,1024]{1,0:T(8,128)(2,1)S(1)} custom-call(bf16[512,1024]{1,0:T(8,128)(2,1)S(1)} %convolution_convert_fusion.6.x_ref), custom_call_target="tpu_custom_call" | custom-call | tf_op jit(solution)/shard_map/line_total/pallas_call | solution.py:262
  524.1 4.3 copy.145
  528.5 4.7 pad_maximum_fusion.1
  533.2 4.7 pad_maximum_fusion
  538.0 3.6 add_add_fusion.4
  543.9 35.5 %reduce-scatter.13.cloned.1.call-done = bf16[128,1152]{1,0:T(8,128)(2,1)} async-done(((bf16[1024,1152]{1,0:T(8,128)(2,1)}), bf16[128,1152]{1,0:T(8,128)(2,1)}) %reduce-scatter.13.cloned.1.call-update) | async-done | bytes 294928
  586.2 47.7 %reduce-scatter.11.cloned.1.call-done = bf16[128,2048]{1,0:T(8,128)(2,1)} async-done(((bf16[1024,2048]{1,0:T(8,128)(2,1)}), bf16[128,2048]{1,0:T(8,128)(2,1)}) %reduce-scatter.11.cloned.1.call-update) | async-done | bytes 524304 | tf_op jit(solution)/shard_map/reduce_scatter | solution.py:375
  635.1 53.3 %reduce-scatter.9.cloned.1.call-done = bf16[128,2048]{1,0:T(8,128)(2,1)} async-done(((bf16[1024,2048]{1,0:T(8,128)(2,1)}), bf16[128,2048]{1,0:T(8,128)(2,1)}) %reduce-scatter.9.cloned.1.call-update) | async-done | bytes 524304 | tf_op jit(solution)/shard_map/reduce_scatter | solution.py:375
  (325 shorter events, 136.3 us)
Async XLA Ops:
  7.2 34.1 %all-gather.7.cloned.1.call-start = ((), (), s32[]{:S(2)}) async-start(), calls=%async_computation.4 | async-start | bytes 2359296 | tf_op jit(solution)/shard_map/all_gather | solution.py:449
  10.4 99.9 %all-gather.9.cloned.1.call-start = ((), (), s32[]{:S(2)}) async-start(), calls=%async_computation.5 | async-start | bytes 4718592 | tf_op jit(solution)/shard_map/all_gather | solution.py:461
  11.4 19.6 %copy-start.18 = (f32[512,1024]{1,0:T(8,128)S(1)}, f32[512,1024]{1,0:T(8,128)}, u32[]{:S(2)}) copy-start(f32[512,1024]{1,0:T(8,128)} %param.12) | copy-start | bytes 6291460
  11.4 144.1 %all-gather.11.cloned.1.call-start = ((), (), s32[]{:S(2)}) async-start(), calls=%async_computation.6 | async-start | bytes 2359296 | tf_op jit(solution)/shard_map/all_gather | solution.py:449
  12.6 212.2 %all-gather.13.cloned.1.call-start = ((), (), s32[]{:S(2)}) async-start(), calls=%async_computation.7 | async-start | bytes 4718592 | tf_op jit(solution)/shard_map/all_gather | solution.py:461
  12.6 37.2 %collective-permute-start.3 = (s32[512]{0:T(512)S(1)}, s32[512]{0:T(512)S(1)}, u32[]{:S(2)}, u32[]{:S(2)}) collective-permute-start(s32[512]{0:T(512)S(1)} %broadcast_add_fusion), channel_id=1, source_target_pairs={{0,4},{4,8},{8,12},{12,16},{16,20},{20,24},{24,28},{1,5},{5,9},{9,... | collective-permute-start | bytes 6152 | tf_op jit(solution)/shard_map/ppermute | solution.py:20
  15.1 34.8 %collective-permute-start.2 = (s32[512]{0:T(512)S(1)}, s32[512]{0:T(512)S(1)}, u32[]{:S(2)}, u32[]{:S(2)}) collective-permute-start(s32[512]{0:T(512)S(1)} %broadcast_add_fusion), channel_id=1, source_target_pairs={{0,8},{4,12},{8,16},{12,20},{16,24},{20,28},{1,9},{5,13},{9,17},{1... | collective-permute-start | bytes 6152 | tf_op jit(solution)/shard_map/ppermute | solution.py:20
  20.3 521.3 %reduce-scatter.15.cloned.1.call-start = ((), (), s32[]{:S(2)}) async-start(), calls=%async_computation.11 | async-start | bytes 2359296
  44.0 8.0 %collective-permute-start.1 = (bf16[512,512]{1,0:T(8,128)(2,1)S(1)}, bf16[512,512]{1,0:T(8,128)(2,1)S(1)}, u32[]{:S(2)}, u32[]{:S(2)}) collective-permute-start(bf16[512,512]{1,0:T(8,128)(2,1)S(1)} %fusion.68), channel_id=1, source_target_pairs={{0,4},{4,8},{8,12},{12,16},{16,20},{20,24},{24,28},{1,5},{5,9},{9,... | collective-permute-start | bytes 1572872 | tf_op jit(solution)/shard_map/ppermute | solution.py:20
  46.3 21.3 %collective-permute-start = (bf16[512,512]{1,0:T(8,128)(2,1)S(1)}, bf16[512,512]{1,0:T(8,128)(2,1)S(1)}, u32[]{:S(2)}, u32[]{:S(2)}) collective-permute-start(bf16[512,512]{1,0:T(8,128)(2,1)S(1)} %fusion.68), channel_id=1, source_target_pairs={{0,8},{4,12},{8,16},{12,20},{16,24},{20,28},{1,9},{5,13},{9,17},{1... | collective-permute-start | bytes 1572872 | tf_op jit(solution)/shard_map/ppermute | solution.py:20
  50.7 21.9 %copy-start.24 = (bf16[32,8,4,256]{3,1,2,0:T(8,128)(2,1)}, bf16[32,8,4,256]{3,1,2,0:T(8,128)(2,1)S(1)}, u32[]{:S(2)}) copy-start(bf16[32,8,4,256]{3,1,2,0:T(8,128)(2,1)S(1)} %copy.154) | copy-start | bytes 1572868
  67.7 41.8 %copy-start = (bf16[1536,512]{1,0:T(8,128)(2,1)}, bf16[1536,512]{1,0:T(8,128)(2,1)S(1)}, u32[]{:S(2)}) copy-start(bf16[1536,512]{1,0:T(8,128)(2,1)S(1)} %pad_maximum_fusion.4.kv_ref) | copy-start | bytes 4718596
  72.6 37.3 %copy-start.6 = (bf16[512,256]{1,0:T(8,128)(2,1)}, bf16[512,256]{1,0:T(8,128)(2,1)S(1)}, u32[]{:S(2)}) copy-start(bf16[512,256]{1,0:T(8,128)(2,1)S(1)} %get-tuple-element.29) | copy-start | bytes 786436
  72.6 37.3 %copy-start.12 = (f32[512,4]{1,0:T(8,128)}, f32[512,4]{1,0:T(8,128)S(1)}, u32[]{:S(2)}) copy-start(f32[512,4]{1,0:T(8,128)S(1)} %get-tuple-element.37.lse_ref) | copy-start | bytes 24580
  72.6 36.9 %copy-start.19 = (f32[512,1024]{1,0:T(8,128)S(1)}, f32[512,1024]{1,0:T(8,128)}, u32[]{:S(2)}) copy-start(f32[512,1024]{1,0:T(8,128)} %param.12) | copy-start | bytes 6291460
  109.8 42.1 %copy-start.16 = (f32[512,1024]{1,0:T(8,128)}, f32[512,1024]{1,0:T(8,128)S(1)}, u32[]{:S(2)}) copy-start(f32[512,1024]{1,0:T(8,128)S(1)} %get-tuple-element.112) | copy-start | bytes 6291460
  158.8 10.0 %collective-permute-start.5 = (bf16[512,512]{1,0:T(8,128)(2,1)S(1)}, bf16[512,512]{1,0:T(8,128)(2,1)S(1)}, u32[]{:S(2)}, u32[]{:S(2)}) collective-permute-start(bf16[512,512]{1,0:T(8,128)(2,1)S(1)} %fusion.67), channel_id=1, source_target_pairs={{0,4},{4,8},{8,12},{12,16},{16,20},{20,24},{24,28},{1,5},{5,9},{9,... | collective-permute-start | bytes 1572872 | tf_op jit(solution)/shard_map/ppermute | solution.py:20
  160.9 17.4 %collective-permute-start.4 = (bf16[512,512]{1,0:T(8,128)(2,1)S(1)}, bf16[512,512]{1,0:T(8,128)(2,1)}, u32[]{:S(2)}, u32[]{:S(2)}) collective-permute-start(bf16[512,512]{1,0:T(8,128)(2,1)S(1)} %fusion.67), channel_id=1, source_target_pairs={{0,8},{4,12},{8,16},{12,20},{16,24},{20,28},{1,9},{5,13},{9,17},{1... | collective-permute-start | bytes 1572872 | tf_op jit(solution)/shard_map/ppermute | solution.py:20
  167.6 17.1 %copy-start.26 = (bf16[32,8,4,256]{3,1,2,0:T(8,128)(2,1)}, bf16[32,8,4,256]{3,1,2,0:T(8,128)(2,1)S(1)}, u32[]{:S(2)}) copy-start(bf16[32,8,4,256]{3,1,2,0:T(8,128)(2,1)S(1)} %copy.155) | copy-start | bytes 1572868
  184.7 38.1 %copy-start.8 = (bf16[512,256]{1,0:T(8,128)(2,1)}, bf16[512,256]{1,0:T(8,128)(2,1)S(1)}, u32[]{:S(2)}) copy-start(bf16[512,256]{1,0:T(8,128)(2,1)S(1)} %get-tuple-element.30) | copy-start | bytes 786436
  184.7 38.1 %copy-start.14 = (f32[512,4]{1,0:T(8,128)}, f32[512,4]{1,0:T(8,128)S(1)}, u32[]{:S(2)}) copy-start(f32[512,4]{1,0:T(8,128)S(1)} %get-tuple-element.31.lse_ref) | copy-start | bytes 24580
  321.2 15.4 %copy-start.22 = (f32[512,1024]{1,0:T(8,128)}, f32[512,1024]{1,0:T(8,128)S(1)}, u32[]{:S(2)}) copy-start(f32[512,1024]{1,0:T(8,128)S(1)} %get-tuple-element.102) | copy-start | bytes 6291460
  322.3 14.3 %copy-start.9 = (bf16[512,256]{1,0:T(8,128)(2,1)S(1)}, bf16[512,256]{1,0:T(8,128)(2,1)}, u32[]{:S(2)}) copy-start(bf16[512,256]{1,0:T(8,128)(2,1)} %copy-done.8) | copy-start | bytes 786436
  333.7 16.7 %collective-permute-start.7 = (bf16[512,512]{1,0:T(8,128)(2,1)}, bf16[512,512]{1,0:T(8,128)(2,1)}, u32[]{:S(2)}, u32[]{:S(2)}) collective-permute-start(bf16[512,512]{1,0:T(8,128)(2,1)} %get-tuple-element.123), channel_id=1, source_target_pairs={{8,0},{12,4},{16,8},{20,12},{24,16},{28,20},{9,1},{13,5},{17,9},{2... | collective-permute-start | bytes 1572872 | tf_op jit(solution)/shard_map/ppermute | solution.py:20
  334.9 15.5 %collective-permute-start.6 = (bf16[512,512]{1,0:T(8,128)(2,1)}, bf16[512,512]{1,0:T(8,128)(2,1)}, u32[]{:S(2)}, u32[]{:S(2)}) collective-permute-start(bf16[512,512]{1,0:T(8,128)(2,1)} %get-tuple-element.122), channel_id=1, source_target_pairs={{4,0},{8,4},{12,8},{16,12},{20,16},{24,20},{28,24},{5,1},{9,5},{13... | collective-permute-start | bytes 1572872 | tf_op jit(solution)/shard_map/ppermute | solution.py:20
  457.4 23.8 %collective-permute-start.9 = (bf16[512,512]{1,0:T(8,128)(2,1)}, bf16[512,512]{1,0:T(8,128)(2,1)}, u32[]{:S(2)}, u32[]{:S(2)}) collective-permute-start(bf16[512,512]{1,0:T(8,128)(2,1)} %get-tuple-element.121), channel_id=1, source_target_pairs={{8,0},{12,4},{16,8},{20,12},{24,16},{28,20},{9,1},{13,5},{17,9},{2... | collective-permute-start | bytes 1572872 | tf_op jit(solution)/shard_map/ppermute | solution.py:20
  458.7 22.6 %collective-permute-start.8 = (bf16[512,512]{1,0:T(8,128)(2,1)}, bf16[512,512]{1,0:T(8,128)(2,1)}, u32[]{:S(2)}, u32[]{:S(2)}) collective-permute-start(bf16[512,512]{1,0:T(8,128)(2,1)} %get-tuple-element.120), channel_id=1, source_target_pairs={{4,0},{8,4},{12,8},{16,12},{20,16},{24,20},{28,24},{5,1},{9,5},{13... | collective-permute-start | bytes 1572872 | tf_op jit(solution)/shard_map/ppermute | solution.py:20
  464.7 114.6 %reduce-scatter.13.cloned.1.call-start = ((), (), s32[]{:S(2)}) async-start(), calls=%async_computation.10 | async-start | bytes 2654208
  470.1 13.4 %copy-start.41 = (bf16[512,256]{1,0:T(8,128)(2,1)S(1)}, bf16[512,256]{1,0:T(8,128)(2,1)}, u32[]{:S(2)}) copy-start(bf16[512,256]{1,0:T(8,128)(2,1)} %get-tuple-element.125) | copy-start | bytes 786436
  484.5 32.0 %copy-start.20 = (f32[512,1024]{1,0:T(8,128)S(1)}, f32[512,1024]{1,0:T(8,128)}, u32[]{:S(2)}) copy-start(f32[512,1024]{1,0:T(8,128)} %param.12) | copy-start | bytes 6291460
  528.4 105.5 %reduce-scatter.11.cloned.1.call-start = ((), (), s32[]{:S(2)}) async-start(), calls=%async_computation.9 | async-start | bytes 4718592 | tf_op jit(solution)/shard_map/reduce_scatter | solution.py:375
  533.2 155.3 %reduce-scatter.9.cloned.1.call-start = ((), (), s32[]{:S(2)}) async-start(), calls=%async_computation.8 | async-start | bytes 4718592 | tf_op jit(solution)/shard_map/reduce_scatter | solution.py:375
  (41 other events, 186.8 us)
Sparse Core Ops, SparseCore 0:
  10.5 30.8 all-gather.6
  43.8 42.0 all-gather.8
  88.4 28.0 all-gather.10
  118.8 36.5 all-gather.12
  464.8 55.1 reduce-scatter.14
  528.6 50.7 reduce-scatter.12
  582.7 51.1 reduce-scatter.10
  637.3 51.1 reduce-scatter.8
